TPU v7x, 128 devices: a whole 4x4x4 slice. The times are simulated.
128 devices in a mesh: seq: 64 (over z_lo, x, y, core), trace: 2 (over z_hi).
Axes of the slice: x: 4, y: 4, z: 4 (z_hi: 2, z_lo: 2; z = z_hi * 2 + z_lo), core: 2. Of those that a mesh axis runs over, the one named last changes fastest.
Arguments:
- signal: bfloat16 [4, 32768, 256], P('trace', 'seq'), may hold values from -6 to 6
- cotangent: bfloat16 [4, 32768, 256], P('trace', 'seq'), may hold values from -6 to 6
- filter_taps: bfloat16 [32768, 256], P('seq'), may hold values from -6 to 6
Outputs:
- input_grad: float32 [4, 32768, 256], P('trace', 'seq')
- filter_grad: float32 [32768, 256], P('seq')
All inputs are finite; a program needn't handle non-finite values.
Results may differ from a plain program's by a relative error of at most 0.0003.
Values may be sent and summed in bfloat16 or wider, within the bound.
A program may use at most 128 MiB of HBM per device.

v0:
```python
import math

import jax
import jax.numpy as jnp
from jax import lax
from jax.sharding import PartitionSpec as P

HIGHEST = lax.Precision.HIGHEST
THREEPASS = lax.Precision.HIGH


def unit_parts(left_index, right_index, period):
    product = left_index[:, None] * right_index[None, :] % period
    angles = product.astype(jnp.float32) * (2.0 * math.pi / period)
    return (jnp.cos(angles), jnp.sin(angles))


def contract(matrix, operand, pattern, level=HIGHEST):
    return jnp.einsum(pattern, matrix, operand, precision=level, preferred_element_type=jnp.float32)


def steps_of(length):
    return jnp.arange(length, dtype=jnp.int32)


def spectra_by_rows(stacked):
    seq_count = lax.axis_size("seq")
    row_count = stacked.shape[1]
    row_block = row_count // seq_count
    period = 2 * seq_count * row_count
    position = lax.axis_index("seq")
    pieces = lax.all_to_all(stacked, "seq", split_axis=1, concat_axis=1, tiled=True)
    item_count = pieces.shape[0]
    blocks = pieces.astype(jnp.float32).reshape(item_count, seq_count, row_block, pieces.shape[2])
    cos_p, sin_p = unit_parts(steps_of(2 * seq_count), steps_of(seq_count), 2 * seq_count)
    real_part = contract(cos_p, blocks, "jp,bpmc->bjmc", THREEPASS)
    imag_part = -contract(sin_p, blocks, "jp,bpmc->bjmc", THREEPASS)
    cos_t, sin_t = unit_parts(
        steps_of(2 * seq_count), position * row_block + steps_of(row_block), period
    )
    cos_t = cos_t[None, :, :, None]
    sin_t = sin_t[None, :, :, None]
    spec_real = lax.all_to_all(
        real_part * cos_t + imag_part * sin_t, "seq", split_axis=1, concat_axis=2, tiled=True
    )
    spec_imag = lax.all_to_all(
        imag_part * cos_t - real_part * sin_t, "seq", split_axis=1, concat_axis=2, tiled=True
    )
    cos_m, sin_m = unit_parts(steps_of(row_count), steps_of(row_count), row_count)
    out_real = contract(cos_m, spec_real, "rm,bjmc->bcjr") + contract(
        sin_m, spec_imag, "rm,bjmc->bcjr"
    )
    out_imag = contract(cos_m, spec_imag, "rm,bjmc->bcjr") - contract(
        sin_m, spec_real, "rm,bjmc->bcjr"
    )
    return (out_real, out_imag)


def rows_from_spectra(spectrum):
    spec_real, spec_imag = spectrum
    seq_count = lax.axis_size("seq")
    row_count = spec_real.shape[3]
    row_block = row_count // seq_count
    period = 2 * seq_count * row_count
    position = lax.axis_index("seq")
    cos_m, sin_m = unit_parts(steps_of(row_count), steps_of(row_count), row_count)
    back_real = contract(cos_m, spec_real, "mr,bcjr->bjmc") - contract(
        sin_m, spec_imag, "mr,bcjr->bjmc"
    )
    back_imag = contract(sin_m, spec_real, "mr,bcjr->bjmc") + contract(
        cos_m, spec_imag, "mr,bcjr->bjmc"
    )
    part_real = lax.all_to_all(back_real, "seq", split_axis=2, concat_axis=1, tiled=True)
    part_imag = lax.all_to_all(back_imag, "seq", split_axis=2, concat_axis=1, tiled=True)
    cos_t, sin_t = unit_parts(
        steps_of(2 * seq_count), position * row_block + steps_of(row_block), period
    )
    cos_t = cos_t[None, :, :, None]
    sin_t = sin_t[None, :, :, None]
    turned_real = part_real * cos_t - part_imag * sin_t
    turned_imag = part_real * sin_t + part_imag * cos_t
    cos_p, sin_p = unit_parts(steps_of(seq_count), steps_of(2 * seq_count), 2 * seq_count)
    values = contract(cos_p, turned_real, "pj,bjmc->bpmc") - contract(
        sin_p, turned_imag, "pj,bjmc->bpmc"
    )
    spread = values / period
    joined = lax.all_to_all(spread, "seq", split_axis=1, concat_axis=2, tiled=True)
    return joined.reshape(joined.shape[0], row_count, joined.shape[3])


def local(signal, cotangent, filter_taps):
    trace_count = signal.shape[0]
    row_count = signal.shape[1]
    seq_count = lax.axis_size("seq")
    factor = 1.0 / math.sqrt(row_count * seq_count)
    stacked = jnp.concatenate([signal, cotangent, filter_taps[None]], axis=0)
    spec_real, spec_imag = spectra_by_rows(stacked)
    signal_real = spec_real[:trace_count]
    signal_imag = spec_imag[:trace_count]
    upstream_real = spec_real[trace_count : 2 * trace_count]
    upstream_imag = spec_imag[trace_count : 2 * trace_count]
    taps_real = spec_real[2 * trace_count :]
    taps_imag = spec_imag[2 * trace_count :]
    grad_real = (taps_real * upstream_real + taps_imag * upstream_imag) * factor
    grad_imag = (taps_real * upstream_imag - taps_imag * upstream_real) * factor
    input_grad = rows_from_spectra((grad_real, grad_imag))
    sum_real = jnp.sum(signal_real * upstream_real + signal_imag * upstream_imag, axis=0) * factor
    sum_imag = jnp.sum(signal_real * upstream_imag - signal_imag * upstream_real, axis=0) * factor
    sum_real, sum_imag = lax.psum((sum_real, sum_imag), "trace")
    filter_grad = rows_from_spectra((sum_real[None], sum_imag[None]))[0]
    return (input_grad, filter_grad)


def solution(mesh):
    in_specs = (P("trace", "seq", None), P("trace", "seq", None), P("seq", None))
    out_specs = (P("trace", "seq", None), P("seq", None))
    return jax.shard_map(local, mesh=mesh, in_specs=in_specs, out_specs=out_specs, check_vma=False)
```

profile of v0, /device:TPU:1, one launch (start us, length us, event | category | flops | bytes accessed | tf_op | source)
XLA Modules:
  0.0 533.8 jit_solution(11596158510743164570)
XLA Ops:
  13.9 10.3 %all-to-all-start = ((bf16[5,512,256]{2,0,1:T(8,128)(2,1)}), bf16[5,512,256]{2,0,1:T(8,128)(2,1)S(1)}, u32[]{:S(2)}, u32[]{:S(2)}) async-start(bf16[5,512,256]{2,0,1:T(8,128)(2,1)} %pad_maximum_fusion), calls=%async_computation | async-start | bytes 4194304 | tf_op jit(solution)/shard_map/all_to_all | solution.py:32
  24.4 28.3 %all-to-all-done = bf16[5,512,256]{2,0,1:T(8,128)(2,1)S(1)} async-done(((bf16[5,512,256]{2,0,1:T(8,128)(2,1)}), bf16[5,512,256]{2,0,1:T(8,128)(2,1)S(1)}, u32[]{:S(2)}, u32[]{:S(2)}) %all-to-all-start) | async-done | bytes 1310752 | tf_op jit(solution)/shard_map/all_to_all | solution.py:32
  80.0 59.2 %all-to-all-done.2 = f32[5,128,8,256]{3,2,0,1:T(8,128)} async-done(((f32[5,128,8,256]{3,2,0,1:T(8,128)}), f32[5,128,8,256]{3,2,0,1:T(8,128)}, u32[]{:S(2)}, u32[]{:S(2)}) %all-to-all-start.2) | async-done | bytes 5242912 | tf_op jit(solution)/shard_map/all_to_all | solution.py:46
  139.2 14.3 %all-to-all-start.1 = ((f32[5,128,8,256]{3,2,0,1:T(8,128)}), f32[5,128,8,256]{3,2,0,1:T(8,128)}, u32[]{:S(2)}, u32[]{:S(2)}) async-start(f32[5,128,8,256]{3,2,0,1:T(8,128)} %copy.99), calls=%async_computation.1 | async-start | bytes 10485760 | tf_op jit(solution)/shard_map/all_to_all | solution.py:43
  153.5 24.3 %fusion.2 = f32[5,2,256,512]{3,2,1,0:T(8,128)} fusion(f32[5,2,64,8,256]{4,3,0,1,2:T(8,128)} %bitcast.18), kind=kOutput, calls=%fused_computation.2 | convolution fusion | flops 8056733696 | bytes 10485760 | tf_op jit(solution)/shard_map/rm,bjmc->bcjr/dot_general | solution.py:19
  177.8 24.6 %fusion = f32[5,2,256,512]{3,2,1,0:T(8,128)} fusion(f32[5,2,64,8,256]{4,3,0,1,2:T(8,128)} %bitcast.18), kind=kOutput, calls=%fused_computation | convolution fusion | flops 8056733696 | bytes 10485760 | tf_op jit(solution)/shard_map/rm,bjmc->bcjr/dot_general | solution.py:19
  202.4 16.6 %all-to-all-done.1 = f32[5,128,8,256]{3,2,0,1:T(8,128)} async-done(((f32[5,128,8,256]{3,2,0,1:T(8,128)}), f32[5,128,8,256]{3,2,0,1:T(8,128)}, u32[]{:S(2)}, u32[]{:S(2)}) %all-to-all-start.1) | async-done | bytes 5242912 | tf_op jit(solution)/shard_map/all_to_all | solution.py:43
  219.0 27.5 %add_bitcast_fusion = f32[5,256,2,512]{3,1,2,0:T(8,128)S(1)} fusion(f32[5,2,256,512]{3,2,1,0:T(8,128)} %fusion.2, f32[5,2,64,8,256]{4,3,0,1,2:T(8,128)} %bitcast.12), kind=kOutput, calls=%fused_computation.15 | convolution fusion | flops 8058044416 | bytes 15728640 | tf_op jit(solution)/shard_map/rm,bjmc->bcjr/dot_general | solution.py:19
  246.5 25.7 %subtract_bitcast_fusion = f32[5,256,2,512]{3,1,2,0:T(8,128)S(1)} fusion(f32[5,2,256,512]{3,2,1,0:T(8,128)S(1)} %copy-done.2, f32[5,2,64,8,256]{4,3,0,1,2:T(8,128)} %bitcast.12), kind=kOutput, calls=%fused_computation.14 | convolution fusion | flops 8058044416 | bytes 15728640 | tf_op jit(solution)/shard_map/rm,bjmc->bcjr/dot_general | solution.py:19
  272.4 7.8 %fusion.52 = f32[2,256,2,512]{3,1,2,0:T(8,128)S(1)} fusion(f32[5,256,2,512]{3,1,2,0:T(8,128)S(1)} %subtract_bitcast_fusion, f32[5,256,2,512]{3,1,2,0:T(8,128)S(1)} %add_bitcast_fusion, f32[256,2,512]{2,0,1:T(8,128)S(1)} %get-tuple-element.14, f32[256,2,512]{2,0,1:T(8,128)S(1)} %get-tuple-element.15), kind=kOutput, calls=%fused_computation.71 | convolution fusion | flops 3226992640 | bytes 8388608 | tf_op jit(solution)/shard_map/mr,bcjr->bjmc/dot_general | solution.py:19
  280.3 9.1 %subtract_bitcast_fusion.1 = f32[2,2,512,256]{2,3,1,0:T(8,128)} fusion(f32[2,256,2,512]{3,1,2,0:T(8,128)S(1)} %fusion.52, f32[5,256,2,512]{3,1,2,0:T(8,128)S(1)} %subtract_bitcast_fusion, f32[5,256,2,512]{3,1,2,0:T(8,128)S(1)} %add_bitcast_fusion, f32[256,2,512]{2,0,1:T(8,128)S(1)} %get-tuple-element.14, f32[256,2,512]{2,0,1:T(8,128)S(1)} %get-tuple-element.15), kind=kOutput, calls=%fused_computation.32 | convolution fusion | flops 3227516928 | bytes 10485760 | tf_op jit(solution)/shard_map/mr,bcjr->bjmc/dot_general | solution.py:19
  293.5 13.8 %all-to-all-start.3 = ((f32[2,2,512,256]{3,1,0,2:T(2,128)}), f32[2,2,512,256]{3,1,0,2:T(2,128)}, u32[]{:S(2)}, u32[]{:S(2)}) async-start(f32[2,2,512,256]{3,1,0,2:T(2,128)} %copy.109), calls=%async_computation.3 | async-start | bytes 4194304 | tf_op jit(solution)/shard_map/all_to_all | solution.py:73
  314.4 9.8 %fusion.46 = f32[2,256,2,512]{3,1,2,0:T(8,128)S(1)} fusion(f32[5,256,2,512]{3,1,2,0:T(8,128)} %copy-done.1, f32[5,256,2,512]{3,1,2,0:T(8,128)} %copy-done, f32[256,2,512]{2,0,1:T(8,128)S(1)} %get-tuple-element.14, f32[256,2,512]{2,0,1:T(8,128)S(1)} %get-tuple-element.15), kind=kOutput, calls=%fused_computation.65 | convolution fusion | flops 3226992640 | bytes 8388608 | tf_op jit(solution)/shard_map/mr,bcjr->bjmc/dot_general | solution.py:19
  324.1 12.0 %add_bitcast_fusion.1 = f32[2,2,512,256]{2,3,1,0:T(8,128)} fusion(f32[2,256,2,512]{3,1,2,0:T(8,128)S(1)} %fusion.46, f32[5,256,2,512]{3,1,2,0:T(8,128)} %copy-done.1, f32[5,256,2,512]{3,1,2,0:T(8,128)} %copy-done, f32[256,2,512]{2,0,1:T(8,128)S(1)} %get-tuple-element.14, f32[256,2,512]{2,0,1:T(8,128)S(1)} %get-tuple-element.15), kind=kOutput, calls=%fused_computation.31 | convolution fusion | flops 3227516928 | bytes 10485760 | tf_op jit(solution)/shard_map/mr,bcjr->bjmc/dot_general | solution.py:19
  340.3 8.9 %all-to-all-start.4 = ((f32[2,2,512,256]{3,1,0,2:T(2,128)}), f32[2,2,512,256]{3,1,0,2:T(2,128)S(1)}, u32[]{:S(2)}, u32[]{:S(2)}) async-start(f32[2,2,512,256]{3,1,0,2:T(2,128)} %copy.113), calls=%async_computation.4 | async-start | bytes 4194304 | tf_op jit(solution)/shard_map/all_to_all | solution.py:74
  349.2 66.8 %all-reduce.3.cloned.1.call-done = (f32[256,2,512]{2,0,1:T(8,128)}, f32[256,2,512]{2,0,1:T(8,128)}) async-done(((f32[256,2,512]{2,0,1:T(8,128)}, f32[256,2,512]{2,0,1:T(8,128)}), (f32[256,2,512]{2,0,1:T(8,128)}, f32[256,2,512]{2,0,1:T(8,128)})) %all-reduce.3.cloned.1.call-update) | async-done | bytes 2097168 | tf_op jit(solution)/shard_map/psum | solution.py:109
  416.0 7.0 %fusion.44 = f32[256,2,512]{2,0,1:T(8,128)S(1)} fusion(f32[256,2,512]{2,0,1:T(8,128)} %get-tuple-element.4), kind=kOutput, calls=%fused_computation.63 | convolution fusion | flops 1614282752 | bytes 2097152 | tf_op jit(solution)/shard_map/mr,bcjr->bjmc/dot_general | solution.py:19
  430.7 8.4 %all-to-all-start.6 = ((f32[1,2,512,256]{3,1,0,2:T(2,128)}), f32[1,2,512,256]{3,1,0,2:T(2,128)S(1)}, u32[]{:S(2)}, u32[]{:S(2)}) async-start(f32[1,2,512,256]{3,1,0,2:T(2,128)} %copy.121), calls=%async_computation.6 | async-start | bytes 2097152 | tf_op jit(solution)/shard_map/all_to_all | solution.py:73
  444.8 6.3 %fusion.40 = f32[256,2,512]{2,0,1:T(8,128)S(1)} fusion(f32[256,2,512]{2,0,1:T(8,128)S(1)} %copy-done.7), kind=kOutput, calls=%fused_computation.59 | convolution fusion | flops 1614282752 | bytes 2097152 | tf_op jit(solution)/shard_map/mr,bcjr->bjmc/dot_general | solution.py:19
  451.2 6.6 %fusion.31 = f32[1,2,512,256]{2,3,1,0:T(8,128)} fusion(f32[256,2,512]{2,0,1:T(8,128)S(1)} %fusion.40, f32[256,2,512]{2,0,1:T(8,128)S(1)} %copy-done.6), kind=kOutput, calls=%fused_computation.42 | convolution fusion | flops 1614544896 | bytes 3145728 | tf_op jit(solution)/shard_map/mr,bcjr->bjmc/dot_general | solution.py:19
  460.2 9.5 %all-to-all-start.7 = ((f32[1,2,512,256]{3,1,0,2:T(2,128)}), f32[1,2,512,256]{3,1,0,2:T(2,128)}, u32[]{:S(2)}, u32[]{:S(2)}) async-start(f32[1,2,512,256]{3,1,0,2:T(2,128)} %copy.125), calls=%async_computation.7 | async-start | bytes 2097152 | tf_op jit(solution)/shard_map/all_to_all | solution.py:74
  477.3 9.5 %all-to-all-done.7 = f32[1,2,512,256]{3,1,0,2:T(2,128)} async-done(((f32[1,2,512,256]{3,1,0,2:T(2,128)}), f32[1,2,512,256]{3,1,0,2:T(2,128)}, u32[]{:S(2)}, u32[]{:S(2)}) %all-to-all-start.7) | async-done | bytes 1048608 | tf_op jit(solution)/shard_map/all_to_all | solution.py:74
  496.9 12.1 %all-to-all-done.5 = f32[2,64,8,256]{3,2,0,1:T(8,128)S(1)} async-done(((f32[2,64,8,256]{3,2,0,1:T(8,128)}), f32[2,64,8,256]{3,2,0,1:T(8,128)S(1)}, u32[]{:S(2)}, u32[]{:S(2)}) %all-to-all-start.5) | async-done | bytes 1048608 | tf_op jit(solution)/shard_map/all_to_all | solution.py:87
  514.9 10.9 %all-to-all-done.8 = f32[1,64,8,256]{3,2,0,1:T(8,128)S(1)} async-done(((f32[1,64,8,256]{3,2,0,1:T(8,128)}), f32[1,64,8,256]{3,2,0,1:T(8,128)S(1)}, u32[]{:S(2)}, u32[]{:S(2)}) %all-to-all-start.8) | async-done | bytes 524320 | tf_op jit(solution)/shard_map/all_to_all | solution.py:87
  (62 shorter events, 89.6 us)
Async XLA Ops:
  7.2 3.2 copy-start.4
  13.9 38.8 %all-to-all-start = ((bf16[5,512,256]{2,0,1:T(8,128)(2,1)}), bf16[5,512,256]{2,0,1:T(8,128)(2,1)S(1)}, u32[]{:S(2)}, u32[]{:S(2)}) async-start(bf16[5,512,256]{2,0,1:T(8,128)(2,1)} %pad_maximum_fusion), calls=%async_computation | async-start | bytes 4194304 | tf_op jit(solution)/shard_map/all_to_all | solution.py:32
  68.2 70.9 %all-to-all-start.2 = ((f32[5,128,8,256]{3,2,0,1:T(8,128)}), f32[5,128,8,256]{3,2,0,1:T(8,128)}, u32[]{:S(2)}, u32[]{:S(2)}) async-start(f32[5,128,8,256]{3,2,0,1:T(8,128)} %copy.103), calls=%async_computation.2 | async-start | bytes 10485760 | tf_op jit(solution)/shard_map/all_to_all | solution.py:46
  139.2 79.8 %all-to-all-start.1 = ((f32[5,128,8,256]{3,2,0,1:T(8,128)}), f32[5,128,8,256]{3,2,0,1:T(8,128)}, u32[]{:S(2)}, u32[]{:S(2)}) async-start(f32[5,128,8,256]{3,2,0,1:T(8,128)} %copy.99), calls=%async_computation.1 | async-start | bytes 10485760 | tf_op jit(solution)/shard_map/all_to_all | solution.py:43
  219.0 27.5 %copy-start.2 = (f32[5,2,256,512]{3,2,1,0:T(8,128)S(1)}, f32[5,2,256,512]{3,2,1,0:T(8,128)}, u32[]{:S(2)}) copy-start(f32[5,2,256,512]{3,2,1,0:T(8,128)} %fusion) | copy-start | bytes 15728644
  246.5 33.7 %copy-start = (f32[5,256,2,512]{3,1,2,0:T(8,128)}, f32[5,256,2,512]{3,1,2,0:T(8,128)S(1)}, u32[]{:S(2)}) copy-start(f32[5,256,2,512]{3,1,2,0:T(8,128)S(1)} %add_bitcast_fusion) | copy-start | bytes 15728644
  272.2 8.0 %copy-start.1 = (f32[5,256,2,512]{3,1,2,0:T(8,128)}, f32[5,256,2,512]{3,1,2,0:T(8,128)S(1)}, u32[]{:S(2)}) copy-start(f32[5,256,2,512]{3,1,2,0:T(8,128)S(1)} %subtract_bitcast_fusion) | copy-start | bytes 15728644
  293.5 46.8 %all-to-all-start.3 = ((f32[2,2,512,256]{3,1,0,2:T(2,128)}), f32[2,2,512,256]{3,1,0,2:T(2,128)}, u32[]{:S(2)}, u32[]{:S(2)}) async-start(f32[2,2,512,256]{3,1,0,2:T(2,128)} %copy.109), calls=%async_computation.3 | async-start | bytes 4194304 | tf_op jit(solution)/shard_map/all_to_all | solution.py:73
  307.4 108.6 %all-reduce.3.cloned.1.call-start = ((), (), s32[]{:S(2)}) async-start(), calls=%async_computation.9 | async-start | bytes 4194304 | tf_op jit(solution)/shard_map/psum | solution.py:109
  340.3 90.3 %all-to-all-start.4 = ((f32[2,2,512,256]{3,1,0,2:T(2,128)}), f32[2,2,512,256]{3,1,0,2:T(2,128)S(1)}, u32[]{:S(2)}, u32[]{:S(2)}) async-start(f32[2,2,512,256]{3,1,0,2:T(2,128)} %copy.113), calls=%async_computation.4 | async-start | bytes 4194304 | tf_op jit(solution)/shard_map/all_to_all | solution.py:74
  416.0 7.0 %copy-start.5 = (f32[256,2,512]{2,0,1:T(8,128)S(1)}, f32[256,2,512]{2,0,1:T(8,128)}, u32[]{:S(2)}) copy-start(f32[256,2,512]{2,0,1:T(8,128)} %get-tuple-element.5) | copy-start | bytes 3145732
  430.7 29.6 %all-to-all-start.6 = ((f32[1,2,512,256]{3,1,0,2:T(2,128)}), f32[1,2,512,256]{3,1,0,2:T(2,128)S(1)}, u32[]{:S(2)}, u32[]{:S(2)}) async-start(f32[1,2,512,256]{3,1,0,2:T(2,128)} %copy.121), calls=%async_computation.6 | async-start | bytes 2097152 | tf_op jit(solution)/shard_map/all_to_all | solution.py:73
  443.2 1.6 copy-start.7
  444.8 6.3 %copy-start.6 = (f32[256,2,512]{2,0,1:T(8,128)S(1)}, f32[256,2,512]{2,0,1:T(8,128)}, u32[]{:S(2)}) copy-start(f32[256,2,512]{2,0,1:T(8,128)} %get-tuple-element.5) | copy-start | bytes 3145732
  457.8 12.0 %copy-start.3 = (f32[2,64,2,8,256]{4,3,2,1,0:T(8,128)S(1)}, f32[2,64,2,8,256]{4,3,2,1,0:T(8,128)}, u32[]{:S(2)}) copy-start(f32[2,64,2,8,256]{4,3,2,1,0:T(8,128)} %copy.111) | copy-start | bytes 6291460
  460.2 26.6 %all-to-all-start.7 = ((f32[1,2,512,256]{3,1,0,2:T(2,128)}), f32[1,2,512,256]{3,1,0,2:T(2,128)}, u32[]{:S(2)}, u32[]{:S(2)}) async-start(f32[1,2,512,256]{3,1,0,2:T(2,128)} %copy.125), calls=%async_computation.7 | async-start | bytes 2097152 | tf_op jit(solution)/shard_map/all_to_all | solution.py:74
  486.8 22.2 %all-to-all-start.5 = ((f32[2,64,8,256]{3,2,0,1:T(8,128)}), f32[2,64,8,256]{3,2,0,1:T(8,128)S(1)}, u32[]{:S(2)}, u32[]{:S(2)}) async-start(f32[2,64,8,256]{3,2,0,1:T(8,128)} %copy.119), calls=%async_computation.5 | async-start | bytes 2097152 | tf_op jit(solution)/shard_map/all_to_all | solution.py:87
  509.0 16.8 %all-to-all-start.8 = ((f32[1,64,8,256]{3,2,0,1:T(8,128)}), f32[1,64,8,256]{3,2,0,1:T(8,128)S(1)}, u32[]{:S(2)}, u32[]{:S(2)}) async-start(f32[1,64,8,256]{3,2,0,1:T(8,128)} %copy.131), calls=%async_computation.8 | async-start | bytes 1048576 | tf_op jit(solution)/shard_map/all_to_all | solution.py:87
Sparse Core Ops, SparseCore 0:
  314.5 101.5 all-reduce.2
where the time goes:
time: 544 us; the launch traced here: 534 us
  waiting for transfers between devices  203 us (37%)
  matrix products  182 us (33%)
  starting transfers between devices  80.9 us (15%)
  local copies, waits for them, and re-layouts  40.1 us (7%)
  between operations  14.8 us (3%)
  other arithmetic  12.2 us (2%)
    dot_general x18, matrix products, contract(): jnp.einsum(pattern, matrix, operand, precision=level, preferred_element_t...  182 us
    psum x1, waiting for transfers between devices, local(): sum_real, sum_imag = lax.psum((sum_real, sum_imag), 'trace')  66.8 us
    all_to_all x1, waiting for transfers between devices, spectra_by_rows(): lax.all_to_all(imag_part * cos_t - real_part * sin_t, 'seq', split_axis=1...  59.2 us
    all_to_all x1, waiting for transfers between devices, spectra_by_rows(): lax.all_to_all(stacked, 'seq', split_axis=1, concat_axis=1, tiled=True)  28.3 us
    all_to_all x2, waiting for transfers between devices, rows_from_spectra(): lax.all_to_all(spread, 'seq', split_axis=1, concat_axis=2, tiled=True)  23 us
    all_to_all x2, starting transfers between devices, rows_from_spectra(): lax.all_to_all(back_real, 'seq', split_axis=2, concat_axis=1, tiled=True)  22.2 us
    all_to_all x2, starting transfers between devices, rows_from_spectra(): lax.all_to_all(back_imag, 'seq', split_axis=2, concat_axis=1, tiled=True)  18.4 us
    all_to_all x1, waiting for transfers between devices, spectra_by_rows(): lax.all_to_all(real_part * cos_t + imag_part * sin_t, 'seq', split_axis=1...  16.6 us
  transfers between devices with their start and end apart: 10, of which 7 were waited for; matrix products, arithmetic and copies ran while one was open for 26% of the time, Pallas kernels for 0%

commit v1 on v0

v1 whole, which is shorter than its diff:
```python
import math

import jax
import jax.numpy as jnp
import numpy as np
from jax import lax
from jax.experimental import pallas as pl
from jax.experimental.pallas import tpu as pltpu
from jax.sharding import PartitionSpec as P

LANES = 128
STRIDE = 37
MESH = pl.DeviceIdType.MESH
F32 = jnp.float32
BF16 = jnp.bfloat16


def halves(values):
    high = np.asarray(values, np.float32).astype(jnp.bfloat16)
    low = (values - high.astype(np.float64)).astype(jnp.bfloat16)
    return high, low


def tables(seq_count, pieces):
    rows = seq_count * pieces
    length = rows * LANES
    order = (np.arange(seq_count)[None, :] * pieces + np.arange(pieces)[:, None]).reshape(-1)
    odd = np.arange(rows) + 0.5
    angle = 2.0 * math.pi * odd[:, None] * order[None, :] / (2 * rows)
    split = np.concatenate([np.cos(angle), -np.sin(angle)], axis=0)
    scale = (2.0 / (2 * length)) / math.sqrt(length)
    join = np.concatenate([np.cos(angle.T), -np.sin(angle.T)], axis=1) * scale
    turn = 2.0 * math.pi * odd[:, None] * np.arange(LANES)[None, :] / (2 * length)
    inner = 2.0 * math.pi * np.outer(np.arange(LANES), np.arange(LANES)) / LANES
    cos, sin = np.cos(inner), np.sin(inner)
    ahead = np.block([[cos, -sin], [sin, cos]])
    back = np.block([[cos, sin], [-sin, cos]])
    turns = np.stack([np.cos(turn), -np.sin(turn)]).astype(np.float32)
    stack = lambda values: np.stack(halves(values))
    return stack(split), stack(join), stack(ahead), stack(back), turns


def parts_of(values):
    high = values.astype(BF16)
    return high, (values - high.astype(F32)).astype(BF16)


def dot(left, right):
    return jnp.dot(left, right, preferred_element_type=F32)


def kernel(seq_count, trace_groups, cot, taps, sig, split_h, join_h, ahead_h, back_h, turns_h,
           input_out, filter_out, split, join, ahead, back, turns, send_c, send_t, send_s,
           recv_c, recv_t, recv_s, sequences, spectra, out_i, out_f, in_i, in_f,
           const_sem, send_sem, recv_sem):
    total = seq_count * trace_groups
    held, span, channels = cot.shape
    own = channels // total
    pieces = span // LANES
    traces = held * trace_groups
    rows = seq_count * pieces
    seq = lax.axis_index("seq")
    group = lax.axis_index("trace")
    me = group * seq_count + seq
    barrier = pltpu.get_barrier_semaphore()

    consts = [
        pltpu.make_async_copy(src, dst, const_sem.at[n])
        for n, (src, dst) in enumerate(
            [(split_h, split), (join_h, join), (ahead_h, ahead), (back_h, back), (turns_h, turns)]
        )
    ]
    for copy in consts:
        copy.start()

    def place(target):
        return (lax.rem(target, seq_count), lax.div(target, seq_count))

    def other(step):
        return lax.rem(me + step * STRIDE, total)

    def greet(step, carry):
        pl.semaphore_signal(barrier, inc=1, device_id=place(other(step)), device_id_type=MESH)
        return carry

    lax.fori_loop(1, total, greet, 0)

    def spread(block):
        turned = block.T
        return [
            turned[c * total : (c + 1) * total, m * LANES : (m + 1) * LANES]
            for c in range(own)
            for m in range(pieces)
        ]

    def stage(items, target):
        listed = [piece for item in items for piece in spread(item)]
        target[...] = jnp.swapaxes(jnp.stack(listed), 0, 1)

    stage([taps[...]], send_t)
    stage([cot[i] for i in range(held)], send_c)
    stage([sig[i] for i in range(held)], send_s)
    recv_t[seq] = send_t[me]
    recv_c[me] = send_c[me]
    recv_s[me] = send_s[me]
    pl.semaphore_wait(barrier, total - 1)

    def push(source, target, slot, device):
        pltpu.make_async_remote_copy(
            src_ref=source,
            dst_ref=target,
            send_sem=send_sem.at[slot],
            recv_sem=recv_sem.at[slot],
            device_id=place(device),
            device_id_type=MESH,
        ).start()

    def send_taps(step, carry):
        target = group * seq_count + lax.rem(seq + step * STRIDE, seq_count)
        push(send_t.at[target], recv_t.at[seq], 0, target)
        return carry

    def send_cot(step, carry):
        push(send_c.at[other(step)], recv_c.at[me], 1, other(step))
        return carry

    def send_sig(step, carry):
        push(send_s.at[other(step)], recv_s.at[me], 2, other(step))
        return carry

    lax.fori_loop(1, seq_count, send_taps, 0)
    lax.fori_loop(1, total, send_cot, 0)
    lax.fori_loop(1, total, send_sig, 0)

    def arrive(ref, count, slot):
        view = ref.at[pl.ds(0, count)]
        pltpu.make_async_copy(view, view, recv_sem.at[slot]).wait()

    def depart(ref, count, slot):
        view = ref.at[pl.ds(0, count)]
        pltpu.make_async_copy(view, view, send_sem.at[slot]).wait()

    for copy in consts:
        copy.wait()

    def gather(block, count, first):
        moved = jnp.swapaxes(block, 0, 1)
        for i in range(count):
            columns = []
            for c in range(own):
                start = (i * own + c) * pieces
                columns.append(jnp.concatenate([moved[start + m] for m in range(pieces)], axis=0))
            sequences[first + i] = jnp.concatenate(columns, axis=1)

    def ahead_item(n, carry):
        values = sequences[n]
        first = dot(split[0], values) + dot(split[1], values)
        real, imag = first[:rows], first[rows:]
        for c in range(own):
            lanes = slice(c * LANES, (c + 1) * LANES)
            re, im = real[:, lanes], imag[:, lanes]
            turned = jnp.concatenate(
                [re * turns[0] - im * turns[1], re * turns[1] + im * turns[0]], axis=1
            )
            high, low = parts_of(turned)
            spectra[n, c] = dot(high, ahead[0]) + dot(low, ahead[0]) + dot(high, ahead[1])
        return carry

    def back_item(products):
        highs, lows = [], []
        for product in products:
            high, low = parts_of(product)
            mid = dot(high, back[0]) + dot(low, back[0]) + dot(high, back[1])
            re, im = mid[:, :LANES], mid[:, LANES:]
            turned = jnp.concatenate(
                [re * turns[0] + im * turns[1], im * turns[0] - re * turns[1]], axis=0
            )
            high, low = parts_of(turned)
            highs.append(high)
            lows.append(low)
        high = jnp.concatenate(highs, axis=1)
        low = jnp.concatenate(lows, axis=1)
        return dot(join[0], high) + dot(join[0], low) + dot(join[1], high)

    def turned_product(left, right):
        lr, li = left[:, :LANES], left[:, LANES:]
        rr, ri = right[:, :LANES], right[:, LANES:]
        return jnp.concatenate([lr * rr + li * ri, lr * ri - li * rr], axis=1)

    def cut(values):
        return [
            values[m * seq_count : (m + 1) * seq_count, c * LANES : (c + 1) * LANES]
            for c in range(own)
            for m in range(pieces)
        ]

    arrive(recv_t, seq_count - 1, 0)
    gather(recv_t[...], 1, 0)
    arrive(recv_c, total - 1, 1)
    for other_group in range(trace_groups):
        gather(recv_c[other_group * seq_count : (other_group + 1) * seq_count], held,
               1 + other_group * held)
    lax.fori_loop(0, 1 + traces, ahead_item, 0)

    def input_group(other_group, carry):
        listed = []
        for i in range(held):
            n = 1 + other_group * held + i
            listed += cut(back_item([turned_product(spectra[0, c], spectra[n, c]) for c in range(own)]))
        base = pl.multiple_of(other_group * seq_count, seq_count)
        out_i[pl.ds(base, seq_count)] = jnp.swapaxes(jnp.stack(listed), 0, 1)
        return carry

    lax.fori_loop(0, trace_groups, input_group, 0)
    in_i[me] = out_i[me]

    def send_input(step, carry):
        push(out_i.at[other(step)], in_i.at[me], 3, other(step))
        return carry

    lax.fori_loop(1, total, send_input, 0)

    arrive(recv_s, total - 1, 2)
    for other_group in range(trace_groups):
        gather(recv_s[other_group * seq_count : (other_group + 1) * seq_count], held,
               1 + traces + other_group * held)
    lax.fori_loop(1 + traces, 1 + 2 * traces, ahead_item, 0)
    sums = []
    for c in range(own):
        acc = None
        for b in range(traces):
            product = turned_product(spectra[1 + traces + b, c], spectra[1 + b, c])
            acc = product if acc is None else acc + product
        sums.append(acc)
    out_f[...] = jnp.swapaxes(jnp.stack(cut(back_item(sums))), 0, 1)
    in_f[me] = out_f[seq]

    def send_filter(step, carry):
        push(out_f.at[lax.rem(other(step), seq_count)], in_f.at[me], 4, other(step))
        return carry

    lax.fori_loop(1, total, send_filter, 0)

    def settle(block, i):
        return block[i].T

    arrive(in_i, total - 1, 3)
    moved = jnp.swapaxes(in_i[...], 0, 1)
    for i in range(held):
        for c in range(own):
            for m in range(pieces):
                input_out[i, m * LANES : (m + 1) * LANES, c * total : (c + 1) * total] = moved[
                    (i * own + c) * pieces + m
                ].T
    arrive(in_f, total - 1, 4)
    moved = jnp.swapaxes(in_f[...], 0, 1)
    for c in range(own):
        for m in range(pieces):
            filter_out[m * LANES : (m + 1) * LANES, c * total : (c + 1) * total] = moved[
                c * pieces + m
            ].T
    depart(recv_t, seq_count - 1, 0)
    depart(recv_c, total - 1, 1)
    depart(recv_s, total - 1, 2)
    depart(in_i, total - 1, 3)
    depart(in_f, total - 1, 4)


def local(seq_count, trace_groups, signal, cotangent, filter_taps):
    total = seq_count * trace_groups
    held, span, channels = signal.shape
    own = channels // total
    pieces = span // LANES
    rows = seq_count * pieces
    items = 1 + 2 * held * trace_groups
    constants = [jnp.asarray(table) for table in tables(seq_count, pieces)]
    wide, thin = held * own * pieces, own * pieces
    vmem = pl.BlockSpec(memory_space=pltpu.VMEM)
    anywhere = pl.BlockSpec(memory_space=pl.ANY)

    def body(*refs):
        kernel(seq_count, trace_groups, *refs)

    return pl.pallas_call(
        body,
        out_shape=(
            jax.ShapeDtypeStruct((held, span, channels), F32),
            jax.ShapeDtypeStruct((span, channels), F32),
        ),
        in_specs=[vmem] * 3 + [anywhere] * len(constants),
        out_specs=(vmem, vmem),
        scratch_shapes=[pltpu.VMEM(table.shape, table.dtype) for table in constants]
        + [
            pltpu.VMEM((total, wide, LANES), BF16),
            pltpu.VMEM((total, thin, LANES), BF16),
            pltpu.VMEM((total, wide, LANES), BF16),
            pltpu.VMEM((total, wide, LANES), BF16),
            pltpu.VMEM((seq_count, thin, LANES), BF16),
            pltpu.VMEM((total, wide, LANES), BF16),
            pltpu.VMEM((items, rows, own * LANES), BF16),
            pltpu.VMEM((items, own, rows, 2 * LANES), F32),
            pltpu.VMEM((total, wide, LANES), F32),
            pltpu.VMEM((seq_count, thin, LANES), F32),
            pltpu.VMEM((total, wide, LANES), F32),
            pltpu.VMEM((total, thin, LANES), F32),
            pltpu.SemaphoreType.DMA((len(constants),)),
            pltpu.SemaphoreType.DMA((5,)),
            pltpu.SemaphoreType.DMA((5,)),
        ],
        name="correlate",
        compiler_params=pltpu.CompilerParams(
            collective_id=0, has_side_effects=True, vmem_limit_bytes=56 << 20
        ),
    )(cotangent, filter_taps, signal, *constants)


def solution(mesh):
    seq_count, trace_groups = mesh.shape["seq"], mesh.shape["trace"]

    def run(signal, cotangent, filter_taps):
        return local(seq_count, trace_groups, signal, cotangent, filter_taps)

    in_specs = (P("trace", "seq", None), P("trace", "seq", None), P("seq", None))
    out_specs = (P("trace", "seq", None), P("seq", None))
    return jax.shard_map(run, mesh=mesh, in_specs=in_specs, out_specs=out_specs, check_vma=False)
```

time: 544 us -> 59.3 us (0.11); the launches traced: 534 us -> 59.2 us
  waiting for transfers between devices: 203 us -> 0 us
  matrix products: 182 us -> 0 us
  starting transfers between devices: 80.9 us -> 0 us
  Pallas kernels: 0 us -> 55.4 us
  local copies, waits for them, and re-layouts: 40.1 us -> 3.12 us
  between operations: 14.8 us -> 0.65 us
  other arithmetic: 12.2 us -> 0 us
    dot_general x18 -> x0, matrix products: 182 us -> none  [contract(): jnp.einsum(pattern, matrix, operand, precision=level, preferred_element_t...]
    all_to_all x9 -> x0, waiting for transfers between devices: 137 us -> none  [the longest x1 59.2 us: spectra_by_rows(): lax.all_to_all(imag_part * cos_t - real_part * sin_t, 'seq', split_axis=1...]
    all_to_all x9 -> x0, starting transfers between devices: 80.5 us -> none  [the longest x2 22.2 us: rows_from_spectra(): lax.all_to_all(back_real, 'seq', split_axis=2, concat_axis=1, tiled=True)]
    psum x1 -> x0, waiting for transfers between devices: 66.8 us -> none  [local(): sum_real, sum_imag = lax.psum((sum_real, sum_imag), 'trace')]
    pallas_call x0 -> x1, Pallas kernels: none -> 55.4 us  [local(): pl.pallas_call(body, out_shape=(jax.ShapeDtypeStruct((held, span, channel...]
    add x3 -> x0, local copies, waits for them, and re-layouts: 12.7 us -> none  [the longest x2 6.54 us: rows_from_spectra(): contract(sin_m, spec_real, 'mr,bcjr->bjmc')]
    sub x3 -> x0, local copies, waits for them, and re-layouts: 11.7 us -> none  [the longest x1 6.19 us: spectra_by_rows(): imag_part * cos_t - real_part * sin_t]
    all_to_all x9 -> x0, local copies, waits for them, and re-layouts: 8.28 us -> none  [the longest x4 3.78 us: rows_from_spectra(): lax.all_to_all(back_real, 'seq', split_axis=2, concat_axis=1, tiled=True)]
  transfers between devices with their start and end apart: 10 -> 0, of which waited for: 7 -> 0; matrix products, arithmetic and copies ran while one was open for 26% -> 0% of each run, Pallas kernels for 0% -> 0%
where the time goes in v1:
time: 59.3 us; the launch traced here: 59.2 us
  Pallas kernels  55.4 us (93%)
  local copies, waits for them, and re-layouts  3.12 us (5%)
  between operations  0.65 us (1%)
    pallas_call x1, Pallas kernels, local(): pl.pallas_call(body, out_shape=(jax.ShapeDtypeStruct((held, span, channel...  55.4 us
    unnamed x4, local copies, waits for them, and re-layouts  3.12 us

profile of v1, /device:TPU:1, one launch (start us, length us, event | category | flops | bytes accessed | tf_op | source)
XLA Modules:
  0.0 59.2 jit_solution(8441468440111541571)
XLA Ops:
  0.6 55.4 %correlate.1 = (f32[2,512,256]{2,1,0:T(8,128)}, f32[512,256]{1,0:T(8,128)}) custom-call(bf16[2,512,256]{2,1,0:T(8,128)(2,1)} %refs_0_.1, bf16[512,256]{1,0:T(8,128)(2,1)} %refs_1_.1, bf16[2,512,256]{2,1,0:T(8,128)(2,1)} %refs_2_.1, bf16[2,512,256]{2,1,0:T(8,128)(2,1)} %constant.10.clone.refs_3_, bf16[2,256,512]{2,1,0:T(8,128)(2,1)} %constant.11.clone.refs_4_, ...), custom_call_target="tpu_custom_call" | custom-call | tf_op jit(solution)/shard_map/correlate/pallas_call | solution.py:284
  56.1 0.0 copy-start
  56.1 2.3 %copy.12 = f32[2,512,256]{2,1,0:T(8,128)} copy(f32[2,512,256]{2,1,0:T(8,128)} %get-tuple-element.4) | data formatting | bytes 2097152
  58.4 0.0 copy-done
  58.4 0.8 %copy.13 = f32[512,256]{1,0:T(8,128)} copy(f32[512,256]{1,0:T(8,128)S(1)} %copy-done) | data formatting | bytes 1048576
Async XLA Ops:
  56.1 2.3 %copy-start = (f32[512,256]{1,0:T(8,128)S(1)}, f32[512,256]{1,0:T(8,128)}, u32[]{:S(2)}) copy-start(f32[512,256]{1,0:T(8,128)} %get-tuple-element.5) | copy-start | bytes 1572868

commit v2 on v1

v2 whole, which is shorter than its diff:
```python
import math

import jax
import jax.numpy as jnp
import numpy as np
from jax import lax
from jax.experimental import pallas as pl
from jax.experimental.pallas import tpu as pltpu
from jax.sharding import PartitionSpec as P

LANES = 128
STRIDE = 37
POWER = 9
CEILING = 2.0**14
MESH = pl.DeviceIdType.MESH
F32 = jnp.float32
BF16 = jnp.bfloat16


def halves(values):
    high = np.asarray(values, np.float32).astype(jnp.bfloat16)
    low = (values - high.astype(np.float64)).astype(jnp.bfloat16)
    return high, low


def tables(seq_count, pieces):
    rows = seq_count * pieces
    length = rows * LANES
    near = np.arange(rows // 2) + 0.5
    odd = np.concatenate([near, rows - near])
    scale = (2.0 / (2 * length)) / math.sqrt(length)
    splits, joins = [], []
    for parity in range(2):
        order = np.concatenate(
            [np.arange(seq_count) * pieces + m for m in range(parity, pieces, 2)]
        )
        angle = 2.0 * math.pi * near[:, None] * order[None, :] / (2 * rows)
        high, low = halves(np.concatenate([np.cos(angle), -np.sin(angle)], axis=0))
        splits.append(np.concatenate([high, low], axis=1))
        joins.append(
            np.stack(halves(np.concatenate([np.cos(angle.T), -np.sin(angle.T)], axis=1) * scale))
        )
    turn = 2.0 * math.pi * odd[:, None] * np.arange(LANES)[None, :] / (2 * length)
    inner = 2.0 * math.pi * np.outer(np.arange(LANES), np.arange(LANES)) / LANES
    cos, sin = np.cos(inner), np.sin(inner)
    ahead = np.block([[cos, -sin], [sin, cos]])
    back = np.block([[cos, sin], [-sin, cos]])
    turns = np.stack([np.cos(turn), -np.sin(turn)]).astype(np.float32)
    return np.stack(splits), np.stack(joins), np.stack(halves(ahead)), np.stack(halves(back)), turns


def parts_of(values):
    high = values.astype(BF16)
    return high, (values - high.astype(F32)).astype(BF16)


def dot(left, right):
    return jnp.dot(left, right, preferred_element_type=F32)


def kernel(seq_count, trace_groups, near_count, cot_h, taps_h, sig_h, split_h, join_h, ahead_h,
           back_h, turns_h, input_out, filter_out, cot, taps, sig, split, join, ahead, back, turns,
           send_c, send_t, send_s, recv_c, recv_t, recv_s, peak, peaks_near, peak_far, peaks_far,
           sequences, spectra, out_i, out_f, in_i, in_f, done_i, done_f,
           load_sem, store_sem, send_sem, recv_sem):
    total = seq_count * trace_groups
    held, span, channels = cot.shape
    own = channels // total
    pieces = span // LANES
    traces = held * trace_groups
    rows = seq_count * pieces
    half = rows // 2
    far_count = total // near_count
    seq = lax.axis_index("seq")
    group = lax.axis_index("trace")
    me = group * seq_count + seq
    barrier = pltpu.get_barrier_semaphore()

    loads = [
        pltpu.make_async_copy(src, dst, load_sem.at[n])
        for n, (src, dst) in enumerate(
            [(cot_h, cot), (taps_h, taps), (sig_h, sig), (split_h, split), (join_h, join),
             (ahead_h, ahead), (back_h, back), (turns_h, turns)]
        )
    ]
    for copy in loads:
        copy.start()

    def place(target):
        return (lax.rem(target, seq_count), lax.div(target, seq_count))

    def other(step):
        return lax.rem(me + step * STRIDE, total)

    def greet(step, carry):
        pl.semaphore_signal(barrier, inc=1, device_id=place(other(step)), device_id_type=MESH)
        return carry

    lax.fori_loop(1, total, greet, 0)

    def spread(block):
        turned = block.T
        return [
            turned[c * total : (c + 1) * total, m * LANES : (m + 1) * LANES]
            for c in range(own)
            for m in range(pieces)
        ]

    def stage(items, target):
        listed = [piece for item in items for piece in spread(item)]
        target[...] = jnp.swapaxes(jnp.stack(listed), 0, 1)

    def largest(values):
        return jnp.max(jnp.abs(values.astype(F32)))

    for copy in loads[:3]:
        copy.wait()
    stage([taps[...]], send_t)
    stage([cot[i] for i in range(held)], send_c)
    stage([sig[i] for i in range(held)], send_s)
    recv_t[seq] = send_t[me]
    recv_c[me] = send_c[me]
    recv_s[me] = send_s[me]
    lane = lax.broadcasted_iota(jnp.int32, (1, LANES), 1)
    peak[...] = jnp.where(
        lane == 0, largest(cot[...]), jnp.where(lane == 1, largest(taps[...]), largest(sig[...]))
    )
    first = lax.div(me, near_count)
    second = lax.rem(me, near_count)
    peaks_near[second] = peak[...]
    pl.semaphore_wait(barrier, total - 1)

    def push(source, target, slot, device):
        pltpu.make_async_remote_copy(
            src_ref=source,
            dst_ref=target,
            send_sem=send_sem.at[slot],
            recv_sem=recv_sem.at[slot],
            device_id=place(device),
            device_id_type=MESH,
        ).start()

    def send_near(step, carry):
        target = first * near_count + lax.rem(second + step, near_count)
        push(peak, peaks_near.at[second], 5, target)
        return carry

    def send_far(step, carry):
        target = lax.rem(first + step, far_count) * near_count + second
        push(peak_far, peaks_far.at[first], 6, target)
        return carry

    def send_taps(step, carry):
        target = group * seq_count + lax.rem(seq + step * STRIDE, seq_count)
        push(send_t.at[target], recv_t.at[seq], 0, target)
        return carry

    def send_cot(step, carry):
        push(send_c.at[other(step)], recv_c.at[me], 1, other(step))
        return carry

    def send_sig(step, carry):
        push(send_s.at[other(step)], recv_s.at[me], 2, other(step))
        return carry

    def arrive(ref, count, slot):
        view = ref.at[pl.ds(0, count)]
        pltpu.make_async_copy(view, view, recv_sem.at[slot]).wait()

    def depart(ref, count, slot):
        view = ref.at[pl.ds(0, count)]
        pltpu.make_async_copy(view, view, send_sem.at[slot]).wait()

    lax.fori_loop(1, near_count, send_near, 0)
    lax.fori_loop(1, seq_count, send_taps, 0)
    lax.fori_loop(1, total, send_cot, 0)
    arrive(peaks_near, near_count - 1, 5)
    peak_far[...] = jnp.max(peaks_near[...], axis=0)
    peaks_far[first] = peak_far[...]
    lax.fori_loop(1, far_count, send_far, 0)
    lax.fori_loop(1, total, send_sig, 0)
    for copy in loads[3:]:
        copy.wait()

    def gather(block, count, start):
        moved = jnp.swapaxes(block, 0, 1)
        for i in range(count):
            for parity in range(2):
                columns = []
                for c in range(own):
                    base = (i * own + c) * pieces
                    columns.append(
                        jnp.concatenate(
                            [moved[base + m] for m in range(parity, pieces, 2)], axis=0
                        )
                    )
                sequences[start + i, parity] = jnp.concatenate(columns, axis=1)

    def ahead_item(n, carry):
        sides = []
        for parity in range(2):
            values = sequences[n, parity]
            sides.append(dot(split[parity], jnp.concatenate([values, values], axis=0)))
        even_re, even_im = sides[0][:half], sides[0][half:]
        odd_re, odd_im = sides[1][:half], sides[1][half:]
        real = jnp.concatenate([even_re + odd_re, even_re - odd_re], axis=0)
        imag = jnp.concatenate([even_im + odd_im, odd_im - even_im], axis=0)
        for c in range(own):
            lanes = slice(c * LANES, (c + 1) * LANES)
            re, im = real[:, lanes], imag[:, lanes]
            turned = jnp.concatenate(
                [re * turns[0] - im * turns[1], re * turns[1] + im * turns[0]], axis=1
            )
            high, low = parts_of(turned)
            spectra[n, c] = dot(high, ahead[0]) + dot(low, ahead[0]) + dot(high, ahead[1])
        return carry

    def back_item(products):
        sides = [[], []]
        for product in products:
            high, low = parts_of(product)
            mid = dot(high, back[0]) + dot(low, back[0]) + dot(high, back[1])
            re, im = mid[:, :LANES], mid[:, LANES:]
            real = re * turns[0] + im * turns[1]
            imag = im * turns[0] - re * turns[1]
            sides[0].append(
                jnp.concatenate([real[:half] + real[half:], imag[:half] - imag[half:]], axis=0)
            )
            sides[1].append(
                jnp.concatenate([real[:half] - real[half:], imag[:half] + imag[half:]], axis=0)
            )
        results = []
        for parity in range(2):
            high, low = parts_of(jnp.concatenate(sides[parity], axis=1))
            results.append(
                dot(join[parity, 0], high) + dot(join[parity, 0], low) + dot(join[parity, 1], high)
            )
        return results

    def turned_product(left, right):
        lr, li = left[:, :LANES], left[:, LANES:]
        rr, ri = right[:, :LANES], right[:, LANES:]
        return jnp.concatenate([lr * rr + li * ri, lr * ri - li * rr], axis=1)

    def cut(sides):
        return [
            sides[m % 2][
                (m // 2) * seq_count : (m // 2 + 1) * seq_count, c * LANES : (c + 1) * LANES
            ]
            for c in range(own)
            for m in range(pieces)
        ]

    def encode(values, inverse):
        scaled = values * (1.0 / inverse)
        square = scaled * scaled
        fourth = square * square
        return (fourth * fourth * scaled).astype(BF16)

    def decode(coded, inverse):
        values = coded.astype(F32)
        size = jnp.abs(values)
        root = jnp.exp2(jnp.log2(size) * (1.0 / POWER)) * inverse
        root = jnp.where(size > 0.0, root, 0.0)
        return jnp.where(values < 0.0, -root, root)

    arrive(recv_t, seq_count - 1, 0)
    gather(recv_t[...], 1, 0)
    arrive(recv_c, total - 1, 1)
    for side in range(trace_groups):
        gather(recv_c[side * seq_count : (side + 1) * seq_count], held, 1 + side * held)
    lax.fori_loop(0, 1 + traces, ahead_item, 0)

    arrive(peaks_far, far_count - 1, 6)
    bounds = jnp.max(peaks_far[...], axis=0)

    def bound(position):
        return jnp.max(jnp.where(lane == position, bounds, 0.0), axis=1, keepdims=True)

    reach = math.sqrt(seq_count * span) / CEILING
    inverse_i = jnp.maximum(bound(0) * bound(1) * reach, 2.0**-120)
    inverse_f = jnp.maximum(bound(0) * bound(2) * (reach * traces), 2.0**-120)

    def input_group(side, carry):
        listed = []
        for i in range(held):
            n = 1 + side * held + i
            sides = back_item([turned_product(spectra[0, c], spectra[n, c]) for c in range(own)])
            listed += cut([encode(values, inverse_i) for values in sides])
        base = pl.multiple_of(side * seq_count, seq_count)
        out_i[pl.ds(base, seq_count)] = jnp.swapaxes(jnp.stack(listed), 0, 1)

        def send_input(step, carry):
            target = side * seq_count + lax.rem(seq + step * STRIDE, seq_count)

            @pl.when(target != me)
            def _():
                push(out_i.at[target], in_i.at[me], 3, target)

            return carry

        lax.fori_loop(0, seq_count, send_input, 0)
        return carry

    lax.fori_loop(0, trace_groups, input_group, 0)
    in_i[me] = out_i[me]

    arrive(recv_s, total - 1, 2)
    for side in range(trace_groups):
        gather(recv_s[side * seq_count : (side + 1) * seq_count], held, 1 + traces + side * held)
    lax.fori_loop(1 + traces, 1 + 2 * traces, ahead_item, 0)
    sums = []
    for c in range(own):
        acc = None
        for b in range(traces):
            product = turned_product(spectra[1 + traces + b, c], spectra[1 + b, c])
            acc = product if acc is None else acc + product
        sums.append(acc)
    coded = cut([encode(values, inverse_f) for values in back_item(sums)])
    out_f[...] = jnp.swapaxes(jnp.stack(coded), 0, 1)
    in_f[me] = out_f[seq]

    def send_filter(step, carry):
        push(out_f.at[lax.rem(other(step), seq_count)], in_f.at[me], 4, other(step))
        return carry

    lax.fori_loop(1, total, send_filter, 0)

    arrive(in_i, total - 1, 3)
    moved = jnp.swapaxes(in_i[...], 0, 1)
    for i in range(held):
        for c in range(own):
            for m in range(pieces):
                done_i[i, m * LANES : (m + 1) * LANES, c * total : (c + 1) * total] = decode(
                    moved[(i * own + c) * pieces + m], inverse_i
                ).T
    store_i = pltpu.make_async_copy(done_i, input_out, store_sem.at[0])
    store_i.start()
    arrive(in_f, total - 1, 4)
    moved = jnp.swapaxes(in_f[...], 0, 1)
    for c in range(own):
        for m in range(pieces):
            done_f[m * LANES : (m + 1) * LANES, c * total : (c + 1) * total] = decode(
                moved[c * pieces + m], inverse_f
            ).T
    store_f = pltpu.make_async_copy(done_f, filter_out, store_sem.at[1])
    store_f.start()
    depart(recv_t, seq_count - 1, 0)
    depart(recv_c, total - 1, 1)
    depart(recv_s, total - 1, 2)
    depart(in_i, total - 1, 3)
    depart(in_f, total - 1, 4)
    depart(peaks_near, near_count - 1, 5)
    depart(peaks_far, far_count - 1, 6)
    store_i.wait()
    store_f.wait()


def local(seq_count, trace_groups, signal, cotangent, filter_taps):
    total = seq_count * trace_groups
    held, span, channels = signal.shape
    own = channels // total
    pieces = span // LANES
    rows = seq_count * pieces
    items = 1 + 2 * held * trace_groups
    near_count = min(16, total // 2)
    constants = [jnp.asarray(table) for table in tables(seq_count, pieces)]
    wide, thin = held * own * pieces, own * pieces
    inputs = [cotangent, filter_taps, signal, *constants]
    anywhere = pl.BlockSpec(memory_space=pl.ANY)

    def body(*refs):
        kernel(seq_count, trace_groups, near_count, *refs)

    return pl.pallas_call(
        body,
        out_shape=(
            jax.ShapeDtypeStruct((held, span, channels), F32),
            jax.ShapeDtypeStruct((span, channels), F32),
        ),
        in_specs=[anywhere] * len(inputs),
        out_specs=(anywhere, anywhere),
        scratch_shapes=[pltpu.VMEM(array.shape, array.dtype) for array in inputs]
        + [
            pltpu.VMEM((total, wide, LANES), BF16),
            pltpu.VMEM((total, thin, LANES), BF16),
            pltpu.VMEM((total, wide, LANES), BF16),
            pltpu.VMEM((total, wide, LANES), BF16),
            pltpu.VMEM((seq_count, thin, LANES), BF16),
            pltpu.VMEM((total, wide, LANES), BF16),
            pltpu.VMEM((1, LANES), F32),
            pltpu.VMEM((near_count, 1, LANES), F32),
            pltpu.VMEM((1, LANES), F32),
            pltpu.VMEM((total // near_count, 1, LANES), F32),
            pltpu.VMEM((items, 2, rows // 2, own * LANES), BF16),
            pltpu.VMEM((items, own, rows, 2 * LANES), F32),
            pltpu.VMEM((total, wide, LANES), BF16),
            pltpu.VMEM((seq_count, thin, LANES), BF16),
            pltpu.VMEM((total, wide, LANES), BF16),
            pltpu.VMEM((total, thin, LANES), BF16),
            pltpu.VMEM((held, span, channels), F32),
            pltpu.VMEM((span, channels), F32),
            pltpu.SemaphoreType.DMA((len(inputs),)),
            pltpu.SemaphoreType.DMA((2,)),
            pltpu.SemaphoreType.DMA((7,)),
            pltpu.SemaphoreType.DMA((7,)),
        ],
        name="correlate",
        compiler_params=pltpu.CompilerParams(
            collective_id=0, has_side_effects=True, vmem_limit_bytes=32 << 20
        ),
    )(*[pltpu.with_memory_space_constraint(x, pltpu.HBM) for x in inputs])


def solution(mesh):
    seq_count, trace_groups = mesh.shape["seq"], mesh.shape["trace"]

    def run(signal, cotangent, filter_taps):
        return local(seq_count, trace_groups, signal, cotangent, filter_taps)

    in_specs = (P("trace", "seq", None), P("trace", "seq", None), P("seq", None))
    out_specs = (P("trace", "seq", None), P("seq", None))
    return jax.shard_map(run, mesh=mesh, in_specs=in_specs, out_specs=out_specs, check_vma=False)
```

time: 59.3 us -> 46.8 us (0.79)
  Pallas kernels: 55.4 us -> 44.3 us
  local copies, waits for them, and re-layouts: 3.12 us -> 1.77 us
    pallas_call x1, Pallas kernels: 55.4 us -> 44.3 us  [local(): pl.pallas_call(body, out_shape=(jax.ShapeDtypeStruct((held, span, channel...]
    unnamed x4 -> x2, local copies, waits for them, and re-layouts: 3.12 us -> 1.77 us
where the time goes in v2:
time: 46.8 us; the launch traced here: 46.7 us
  Pallas kernels  44.3 us (95%)
  local copies, waits for them, and re-layouts  1.77 us (4%)
  between operations  0.64 us (1%)
    pallas_call x1, Pallas kernels, local(): pl.pallas_call(body, out_shape=(jax.ShapeDtypeStruct((held, span, channel...  44.3 us
    unnamed x2, local copies, waits for them, and re-layouts  1.77 us

profile of v2, /device:TPU:1, one launch (start us, length us, event | category | flops | bytes accessed | tf_op | source)
XLA Modules:
  0.0 46.7 jit_solution(13617752027994070339)
XLA Ops:
  0.6 44.3 %correlate.1 = (f32[2,512,256]{2,1,0:T(8,128)S(1)}, f32[512,256]{1,0:T(8,128)S(1)}) custom-call(bf16[2,512,256]{2,1,0:T(8,128)(2,1)} %refs_0_.1, bf16[512,256]{1,0:T(8,128)(2,1)} %refs_1_.1, bf16[2,512,256]{2,1,0:T(8,128)(2,1)} %refs_2_.1, bf16[2,256,256]{2,1,0:T(8,128)(2,1)} %constant.10.clone.refs_3_, bf16[2,2,128,256]{3,2,1,0:T(8,128)(2,1)} %constant.11.clone.refs_4_, ...), custom_call_target="tpu_custom_call" | custom-call | tf_op jit(solution)/shard_map/correlate/pallas_call | solution.py:375
  44.9 1.0 %copy.12 = f32[2,512,256]{2,1,0:T(8,128)} copy(f32[2,512,256]{2,1,0:T(8,128)S(1)} %get-tuple-element.4) | data formatting | bytes 2097152
  45.9 0.8 %copy.13 = f32[512,256]{1,0:T(8,128)} copy(f32[512,256]{1,0:T(8,128)S(1)} %get-tuple-element.5) | data formatting | bytes 1048576

commit v3 on v2

--- a/solution.py
+++ b/solution.py
@@ -12,7 +12,8 @@
 STRIDE = 37
 POWER = 9
 CEILING = 2.0**14
-MESH = pl.DeviceIdType.MESH
+UNROLL = 8
+LOGICAL = pl.DeviceIdType.LOGICAL
 F32 = jnp.float32
 BF16 = jnp.bfloat16
 
@@ -58,6 +59,19 @@
     return jnp.dot(left, right, preferred_element_type=F32)
 
 
+def sweep(start, stop, action):
+    groups = (stop - start) // UNROLL
+
+    def batch(index, carry):
+        for k in range(UNROLL):
+            action(start + index * UNROLL + k)
+        return carry
+
+    lax.fori_loop(0, groups, batch, 0)
+    for step in range(start + groups * UNROLL, stop):
+        action(step)
+
+
 def kernel(seq_count, trace_groups, near_count, cot_h, taps_h, sig_h, split_h, join_h, ahead_h,
            back_h, turns_h, input_out, filter_out, cot, taps, sig, split, join, ahead, back, turns,
            send_c, send_t, send_s, recv_c, recv_t, recv_s, peak, peaks_near, peak_far, peaks_far,
@@ -73,7 +87,7 @@
     far_count = total // near_count
     seq = lax.axis_index("seq")
     group = lax.axis_index("trace")
-    me = group * seq_count + seq
+    me = seq * trace_groups + group
     barrier = pltpu.get_barrier_semaphore()
 
     loads = [
@@ -86,41 +100,36 @@
     for copy in loads:
         copy.start()
 
-    def place(target):
-        return (lax.rem(target, seq_count), lax.div(target, seq_count))
-
     def other(step):
         return lax.rem(me + step * STRIDE, total)
 
-    def greet(step, carry):
-        pl.semaphore_signal(barrier, inc=1, device_id=place(other(step)), device_id_type=MESH)
-        return carry
-
-    lax.fori_loop(1, total, greet, 0)
+    def along(step):
+        return lax.rem(seq + step * STRIDE, seq_count)
+
+    sweep(1, total, lambda step: pl.semaphore_signal(
+        barrier, inc=1, device_id=other(step), device_id_type=LOGICAL))
 
     def spread(block):
         turned = block.T
-        return [
+        listed = [
             turned[c * total : (c + 1) * total, m * LANES : (m + 1) * LANES]
             for c in range(own)
             for m in range(pieces)
         ]
-
-    def stage(items, target):
-        listed = [piece for item in items for piece in spread(item)]
-        target[...] = jnp.swapaxes(jnp.stack(listed), 0, 1)
+        return jnp.swapaxes(jnp.stack(listed), 0, 1)
 
     def largest(values):
         return jnp.max(jnp.abs(values.astype(F32)))
 
     for copy in loads[:3]:
         copy.wait()
-    stage([taps[...]], send_t)
-    stage([cot[i] for i in range(held)], send_c)
-    stage([sig[i] for i in range(held)], send_s)
+    send_t[...] = spread(taps[...])
     recv_t[seq] = send_t[me]
-    recv_c[me] = send_c[me]
-    recv_s[me] = send_s[me]
+    for i in range(held):
+        send_c[i] = spread(cot[i])
+        recv_c[i, me] = send_c[i, me]
+        send_s[i] = spread(sig[i])
+        recv_s[i, me] = send_s[i, me]
     lane = lax.broadcasted_iota(jnp.int32, (1, LANES), 1)
     peak[...] = jnp.where(
         lane == 0, largest(cot[...]), jnp.where(lane == 1, largest(taps[...]), largest(sig[...]))
@@ -136,32 +145,9 @@
             dst_ref=target,
             send_sem=send_sem.at[slot],
             recv_sem=recv_sem.at[slot],
-            device_id=place(device),
-            device_id_type=MESH,
+            device_id=device,
+            device_id_type=LOGICAL,
         ).start()
-
-    def send_near(step, carry):
-        target = first * near_count + lax.rem(second + step, near_count)
-        push(peak, peaks_near.at[second], 5, target)
-        return carry
-
-    def send_far(step, carry):
-        target = lax.rem(first + step, far_count) * near_count + second
-        push(peak_far, peaks_far.at[first], 6, target)
-        return carry
-
-    def send_taps(step, carry):
-        target = group * seq_count + lax.rem(seq + step * STRIDE, seq_count)
-        push(send_t.at[target], recv_t.at[seq], 0, target)
-        return carry
-
-    def send_cot(step, carry):
-        push(send_c.at[other(step)], recv_c.at[me], 1, other(step))
-        return carry
-
-    def send_sig(step, carry):
-        push(send_s.at[other(step)], recv_s.at[me], 2, other(step))
-        return carry
 
     def arrive(ref, count, slot):
         view = ref.at[pl.ds(0, count)]
@@ -171,32 +157,58 @@
         view = ref.at[pl.ds(0, count)]
         pltpu.make_async_copy(view, view, send_sem.at[slot]).wait()
 
-    lax.fori_loop(1, near_count, send_near, 0)
-    lax.fori_loop(1, seq_count, send_taps, 0)
-    lax.fori_loop(1, total, send_cot, 0)
-    arrive(peaks_near, near_count - 1, 5)
+    taps_slot, near_slot, far_slot, filter_slot, input_slot = range(5)
+    cot_slot = 5
+    sig_slot = 5 + held
+
+    def send_near(step):
+        push(peak, peaks_near.at[second], near_slot,
+             first * near_count + lax.rem(second + step, near_count))
+
+    def send_far(step):
+        push(peak_far, peaks_far.at[first], far_slot,
+             lax.rem(first + step, far_count) * near_count + second)
+
+    def send_taps(step):
+        target = along(step) * trace_groups + group
+        push(send_t.at[target], recv_t.at[seq], taps_slot, target)
+
+    def send_cot(i):
+        return lambda step: push(
+            send_c.at[i, other(step)], recv_c.at[i, me], cot_slot + i, other(step))
+
+    def send_sig(i):
+        return lambda step: push(
+            send_s.at[i, other(step)], recv_s.at[i, me], sig_slot + i, other(step))
+
+    sweep(1, near_count, send_near)
+    sweep(1, seq_count, send_taps)
+    for i in range(held):
+        sweep(1, total, send_cot(i))
+    arrive(peaks_near, near_count - 1, near_slot)
     peak_far[...] = jnp.max(peaks_near[...], axis=0)
     peaks_far[first] = peak_far[...]
-    lax.fori_loop(1, far_count, send_far, 0)
-    lax.fori_loop(1, total, send_sig, 0)
+    sweep(1, far_count, send_far)
+    for i in range(held):
+        sweep(1, total, send_sig(i))
     for copy in loads[3:]:
         copy.wait()
 
-    def gather(block, count, start):
+    def gather(block, item):
         moved = jnp.swapaxes(block, 0, 1)
-        for i in range(count):
-            for parity in range(2):
-                columns = []
-                for c in range(own):
-                    base = (i * own + c) * pieces
-                    columns.append(
-                        jnp.concatenate(
-                            [moved[base + m] for m in range(parity, pieces, 2)], axis=0
-                        )
-                    )
-                sequences[start + i, parity] = jnp.concatenate(columns, axis=1)
-
-    def ahead_item(n, carry):
+        for parity in range(2):
+            columns = [
+                jnp.concatenate([moved[c * pieces + m] for m in range(parity, pieces, 2)], axis=0)
+                for c in range(own)
+            ]
+            sequences[item, parity] = jnp.concatenate(columns, axis=1)
+
+    def gather_groups(blocks, item):
+        blocks = blocks.reshape((seq_count, trace_groups) + blocks.shape[1:])
+        for side in range(trace_groups):
+            gather(blocks[:, side], item + side)
+
+    def ahead_first(n):
         sides = []
         for parity in range(2):
             values = sequences[n, parity]
@@ -205,15 +217,25 @@
         odd_re, odd_im = sides[1][:half], sides[1][half:]
         real = jnp.concatenate([even_re + odd_re, even_re - odd_re], axis=0)
         imag = jnp.concatenate([even_im + odd_im, odd_im - even_im], axis=0)
+        listed = []
         for c in range(own):
             lanes = slice(c * LANES, (c + 1) * LANES)
             re, im = real[:, lanes], imag[:, lanes]
-            turned = jnp.concatenate(
+            listed.append(parts_of(jnp.concatenate(
                 [re * turns[0] - im * turns[1], re * turns[1] + im * turns[0]], axis=1
-            )
-            high, low = parts_of(turned)
+            )))
+        return listed
+
+    def ahead_second(n, listed):
+        for c, (high, low) in enumerate(listed):
             spectra[n, c] = dot(high, ahead[0]) + dot(low, ahead[0]) + dot(high, ahead[1])
-        return carry
+
+    def ahead_all(start, stop):
+        waiting = ahead_first(start)
+        for n in range(start, stop):
+            following = ahead_first(n + 1) if n + 1 < stop else None
+            ahead_second(n, waiting)
+            waiting = following
 
     def back_item(products):
         sides = [[], []]
@@ -264,14 +286,16 @@
         root = jnp.where(size > 0.0, root, 0.0)
         return jnp.where(values < 0.0, -root, root)
 
-    arrive(recv_t, seq_count - 1, 0)
-    gather(recv_t[...], 1, 0)
-    arrive(recv_c, total - 1, 1)
-    for side in range(trace_groups):
-        gather(recv_c[side * seq_count : (side + 1) * seq_count], held, 1 + side * held)
-    lax.fori_loop(0, 1 + traces, ahead_item, 0)
-
-    arrive(peaks_far, far_count - 1, 6)
+    first_c, first_s = 1, 1 + traces
+    arrive(recv_t, seq_count - 1, taps_slot)
+    gather(recv_t[...], 0)
+    for i in range(held):
+        arrive(recv_c.at[i], total - 1, cot_slot + i)
+        base = first_c + i * trace_groups
+        gather_groups(recv_c[i], base)
+        ahead_all(base if i else 0, base + trace_groups)
+
+    arrive(peaks_far, far_count - 1, far_slot)
     bounds = jnp.max(peaks_far[...], axis=0)
 
     def bound(position):
@@ -281,52 +305,41 @@
     inverse_i = jnp.maximum(bound(0) * bound(1) * reach, 2.0**-120)
     inverse_f = jnp.maximum(bound(0) * bound(2) * (reach * traces), 2.0**-120)
 
-    def input_group(side, carry):
+    for turn in range(trace_groups):
+        side = lax.rem(group + 1 + turn, trace_groups)
         listed = []
         for i in range(held):
-            n = 1 + side * held + i
+            n = first_c + i * trace_groups + side
             sides = back_item([turned_product(spectra[0, c], spectra[n, c]) for c in range(own)])
             listed += cut([encode(values, inverse_i) for values in sides])
-        base = pl.multiple_of(side * seq_count, seq_count)
-        out_i[pl.ds(base, seq_count)] = jnp.swapaxes(jnp.stack(listed), 0, 1)
-
-        def send_input(step, carry):
-            target = side * seq_count + lax.rem(seq + step * STRIDE, seq_count)
-
-            @pl.when(target != me)
-            def _():
-                push(out_i.at[target], in_i.at[me], 3, target)
-
-            return carry
-
-        lax.fori_loop(0, seq_count, send_input, 0)
-        return carry
-
-    lax.fori_loop(0, trace_groups, input_group, 0)
-    in_i[me] = out_i[me]
-
-    arrive(recv_s, total - 1, 2)
-    for side in range(trace_groups):
-        gather(recv_s[side * seq_count : (side + 1) * seq_count], held, 1 + traces + side * held)
-    lax.fori_loop(1 + traces, 1 + 2 * traces, ahead_item, 0)
+        out_i[:, side] = jnp.swapaxes(jnp.stack(listed), 0, 1)
+
+        def send_input(step):
+            target = along(step)
+            push(out_i.at[target, side], in_i.at[me], input_slot, target * trace_groups + side)
+
+        sweep(1 if turn == trace_groups - 1 else 0, seq_count, send_input)
+    in_i[me] = out_i[seq, group]
+
+    for i in range(held):
+        arrive(recv_s.at[i], total - 1, sig_slot + i)
+        base = first_s + i * trace_groups
+        gather_groups(recv_s[i], base)
+        ahead_all(base, base + trace_groups)
     sums = []
     for c in range(own):
         acc = None
         for b in range(traces):
-            product = turned_product(spectra[1 + traces + b, c], spectra[1 + b, c])
+            product = turned_product(spectra[first_s + b, c], spectra[first_c + b, c])
             acc = product if acc is None else acc + product
         sums.append(acc)
     coded = cut([encode(values, inverse_f) for values in back_item(sums)])
     out_f[...] = jnp.swapaxes(jnp.stack(coded), 0, 1)
     in_f[me] = out_f[seq]
-
-    def send_filter(step, carry):
-        push(out_f.at[lax.rem(other(step), seq_count)], in_f.at[me], 4, other(step))
-        return carry
-
-    lax.fori_loop(1, total, send_filter, 0)
-
-    arrive(in_i, total - 1, 3)
+    sweep(1, total, lambda step: push(
+        out_f.at[lax.div(other(step), trace_groups)], in_f.at[me], filter_slot, other(step)))
+
+    arrive(in_i, total - 1, input_slot)
     moved = jnp.swapaxes(in_i[...], 0, 1)
     for i in range(held):
         for c in range(own):
@@ -336,7 +349,7 @@
                 ).T
     store_i = pltpu.make_async_copy(done_i, input_out, store_sem.at[0])
     store_i.start()
-    arrive(in_f, total - 1, 4)
+    arrive(in_f, total - 1, filter_slot)
     moved = jnp.swapaxes(in_f[...], 0, 1)
     for c in range(own):
         for m in range(pieces):
@@ -345,13 +358,14 @@
             ).T
     store_f = pltpu.make_async_copy(done_f, filter_out, store_sem.at[1])
     store_f.start()
-    depart(recv_t, seq_count - 1, 0)
-    depart(recv_c, total - 1, 1)
-    depart(recv_s, total - 1, 2)
-    depart(in_i, total - 1, 3)
-    depart(in_f, total - 1, 4)
-    depart(peaks_near, near_count - 1, 5)
-    depart(peaks_far, far_count - 1, 6)
+    depart(recv_t, seq_count - 1, taps_slot)
+    for i in range(held):
+        depart(recv_c.at[i], total - 1, cot_slot + i)
+        depart(recv_s.at[i], total - 1, sig_slot + i)
+    depart(in_i, total - 1, input_slot)
+    depart(in_f, total - 1, filter_slot)
+    depart(peaks_near, near_count - 1, near_slot)
+    depart(peaks_far, far_count - 1, far_slot)
     store_i.wait()
     store_f.wait()
 
@@ -382,19 +396,19 @@
         out_specs=(anywhere, anywhere),
         scratch_shapes=[pltpu.VMEM(array.shape, array.dtype) for array in inputs]
         + [
-            pltpu.VMEM((total, wide, LANES), BF16),
+            pltpu.VMEM((held, total, thin, LANES), BF16),
             pltpu.VMEM((total, thin, LANES), BF16),
-            pltpu.VMEM((total, wide, LANES), BF16),
-            pltpu.VMEM((total, wide, LANES), BF16),
+            pltpu.VMEM((held, total, thin, LANES), BF16),
+            pltpu.VMEM((held, total, thin, LANES), BF16),
             pltpu.VMEM((seq_count, thin, LANES), BF16),
-            pltpu.VMEM((total, wide, LANES), BF16),
+            pltpu.VMEM((held, total, thin, LANES), BF16),
             pltpu.VMEM((1, LANES), F32),
             pltpu.VMEM((near_count, 1, LANES), F32),
             pltpu.VMEM((1, LANES), F32),
             pltpu.VMEM((total // near_count, 1, LANES), F32),
             pltpu.VMEM((items, 2, rows // 2, own * LANES), BF16),
             pltpu.VMEM((items, own, rows, 2 * LANES), F32),
-            pltpu.VMEM((total, wide, LANES), BF16),
+            pltpu.VMEM((seq_count, trace_groups, wide, LANES), BF16),
             pltpu.VMEM((seq_count, thin, LANES), BF16),
             pltpu.VMEM((total, wide, LANES), BF16),
             pltpu.VMEM((total, thin, LANES), BF16),
@@ -402,8 +416,8 @@
             pltpu.VMEM((span, channels), F32),
             pltpu.SemaphoreType.DMA((len(inputs),)),
             pltpu.SemaphoreType.DMA((2,)),
-            pltpu.SemaphoreType.DMA((7,)),
-            pltpu.SemaphoreType.DMA((7,)),
+            pltpu.SemaphoreType.DMA((5 + 2 * held,)),
+            pltpu.SemaphoreType.DMA((5 + 2 * held,)),
         ],
         name="correlate",
         compiler_params=pltpu.CompilerParams(

time: 46.8 us -> 41.3 us (0.88)
  Pallas kernels: 44.3 us -> 38.8 us
    pallas_call x1, Pallas kernels: 44.3 us -> 38.8 us  [local(): pl.pallas_call(body, out_shape=(jax.ShapeDtypeStruct((held, span, channel...]
where the time goes in v3:
time: 41.3 us; the launch traced here: 41.2 us
  Pallas kernels  38.8 us (94%)
  local copies, waits for them, and re-layouts  1.77 us (4%)
  between operations  0.64 us (2%)
    pallas_call x1, Pallas kernels, local(): pl.pallas_call(body, out_shape=(jax.ShapeDtypeStruct((held, span, channel...  38.8 us
    unnamed x2, local copies, waits for them, and re-layouts  1.77 us

profile of v3, /device:TPU:1, one launch (start us, length us, event | category | flops | bytes accessed | tf_op | source)
XLA Modules:
  0.0 41.2 jit_solution(2656427653506741206)
XLA Ops:
  0.6 38.8 %correlate.1 = (f32[2,512,256]{2,1,0:T(8,128)S(1)}, f32[512,256]{1,0:T(8,128)S(1)}) custom-call(bf16[2,512,256]{2,1,0:T(8,128)(2,1)} %refs_0_.1, bf16[512,256]{1,0:T(8,128)(2,1)} %refs_1_.1, bf16[2,512,256]{2,1,0:T(8,128)(2,1)} %refs_2_.1, bf16[2,256,256]{2,1,0:T(8,128)(2,1)} %constant.10.clone.refs_3_, bf16[2,2,128,256]{3,2,1,0:T(8,128)(2,1)} %constant.11.clone.refs_4_, ...), custom_call_target="tpu_custom_call" | custom-call | tf_op jit(solution)/shard_map/correlate/pallas_call | solution.py:389
  39.4 1.0 %copy.12 = f32[2,512,256]{2,1,0:T(8,128)} copy(f32[2,512,256]{2,1,0:T(8,128)S(1)} %get-tuple-element.4) | data formatting | bytes 2097152
  40.4 0.8 %copy.13 = f32[512,256]{1,0:T(8,128)} copy(f32[512,256]{1,0:T(8,128)S(1)} %get-tuple-element.5) | data formatting | bytes 1048576

commit v4 on v3

--- a/solution.py
+++ b/solution.py
@@ -13,6 +13,8 @@
 POWER = 9
 CEILING = 2.0**14
 UNROLL = 8
+COT_PARTS = 2
+SIG_PARTS = 1
 LOGICAL = pl.DeviceIdType.LOGICAL
 F32 = jnp.float32
 BF16 = jnp.bfloat16
@@ -59,6 +61,14 @@
     return jnp.dot(left, right, preferred_element_type=F32)
 
 
+def decode(coded, inverse):
+    values = coded.astype(F32)
+    size = jnp.abs(values)
+    root = jnp.exp2(jnp.log2(size) * (1.0 / POWER)) * inverse
+    root = jnp.where(size > 0.0, root, 0.0)
+    return jnp.where(values < 0.0, -root, root)
+
+
 def sweep(start, stop, action):
     groups = (stop - start) // UNROLL
 
@@ -73,9 +83,9 @@
 
 
 def kernel(seq_count, trace_groups, near_count, cot_h, taps_h, sig_h, split_h, join_h, ahead_h,
-           back_h, turns_h, input_out, filter_out, cot, taps, sig, split, join, ahead, back, turns,
+           back_h, turns_h, input_out, in_f, scale_out, cot, taps, sig, split, join, ahead, back, turns,
            send_c, send_t, send_s, recv_c, recv_t, recv_s, peak, peaks_near, peak_far, peaks_far,
-           sequences, spectra, out_i, out_f, in_i, in_f, done_i, done_f,
+           sequences, spectra, out_i, out_f, in_i, done_i, scale,
            load_sem, store_sem, send_sem, recv_sem):
     total = seq_count * trace_groups
     held, span, channels = cot.shape
@@ -88,6 +98,7 @@
     seq = lax.axis_index("seq")
     group = lax.axis_index("trace")
     me = seq * trace_groups + group
+    cot_parts, sig_parts = send_c.shape[0], send_s.shape[0]
     barrier = pltpu.get_barrier_semaphore()
 
     loads = [
@@ -109,10 +120,15 @@
     sweep(1, total, lambda step: pl.semaphore_signal(
         barrier, inc=1, device_id=other(step), device_id_type=LOGICAL))
 
-    def spread(block):
-        turned = block.T
+    def part(ref, index, parts):
+        step = held // parts
+        return [ref[i] for i in range(index * step, (index + 1) * step)]
+
+    def spread(blocks):
+        turned = [block.T for block in blocks]
         listed = [
-            turned[c * total : (c + 1) * total, m * LANES : (m + 1) * LANES]
+            block[c * total : (c + 1) * total, m * LANES : (m + 1) * LANES]
+            for block in turned
             for c in range(own)
             for m in range(pieces)
         ]
@@ -120,24 +136,6 @@
 
     def largest(values):
         return jnp.max(jnp.abs(values.astype(F32)))
-
-    for copy in loads[:3]:
-        copy.wait()
-    send_t[...] = spread(taps[...])
-    recv_t[seq] = send_t[me]
-    for i in range(held):
-        send_c[i] = spread(cot[i])
-        recv_c[i, me] = send_c[i, me]
-        send_s[i] = spread(sig[i])
-        recv_s[i, me] = send_s[i, me]
-    lane = lax.broadcasted_iota(jnp.int32, (1, LANES), 1)
-    peak[...] = jnp.where(
-        lane == 0, largest(cot[...]), jnp.where(lane == 1, largest(taps[...]), largest(sig[...]))
-    )
-    first = lax.div(me, near_count)
-    second = lax.rem(me, near_count)
-    peaks_near[second] = peak[...]
-    pl.semaphore_wait(barrier, total - 1)
 
     def push(source, target, slot, device):
         pltpu.make_async_remote_copy(
@@ -159,7 +157,7 @@
 
     taps_slot, near_slot, far_slot, filter_slot, input_slot = range(5)
     cot_slot = 5
-    sig_slot = 5 + held
+    sig_slot = 5 + cot_parts
 
     def send_near(step):
         push(peak, peaks_near.at[second], near_slot,
@@ -181,32 +179,56 @@
         return lambda step: push(
             send_s.at[i, other(step)], recv_s.at[i, me], sig_slot + i, other(step))
 
+    def stage(blocks, send, receive, place):
+        send[...] = spread(blocks)
+        receive[place] = send[me]
+
+    loads[1].wait()
+    stage([taps[...]], send_t, recv_t, seq)
+    loads[0].wait()
+    stage(part(cot, 0, cot_parts), send_c.at[0], recv_c.at[0], me)
+    loads[2].wait()
+    lane = lax.broadcasted_iota(jnp.int32, (1, LANES), 1)
+    peak[...] = jnp.where(
+        lane == 0, largest(cot[...]), jnp.where(lane == 1, largest(taps[...]), largest(sig[...]))
+    )
+    first = lax.div(me, near_count)
+    second = lax.rem(me, near_count)
+    peaks_near[second] = peak[...]
+    pl.semaphore_wait(barrier, total - 1)
     sweep(1, near_count, send_near)
     sweep(1, seq_count, send_taps)
-    for i in range(held):
+    sweep(1, total, send_cot(0))
+    for i in range(1, cot_parts):
+        stage(part(cot, i, cot_parts), send_c.at[i], recv_c.at[i], me)
         sweep(1, total, send_cot(i))
     arrive(peaks_near, near_count - 1, near_slot)
     peak_far[...] = jnp.max(peaks_near[...], axis=0)
     peaks_far[first] = peak_far[...]
     sweep(1, far_count, send_far)
-    for i in range(held):
+    for i in range(sig_parts):
+        stage(part(sig, i, sig_parts), send_s.at[i], recv_s.at[i], me)
         sweep(1, total, send_sig(i))
     for copy in loads[3:]:
         copy.wait()
 
-    def gather(block, item):
+    def gather(block, items):
         moved = jnp.swapaxes(block, 0, 1)
-        for parity in range(2):
-            columns = [
-                jnp.concatenate([moved[c * pieces + m] for m in range(parity, pieces, 2)], axis=0)
-                for c in range(own)
-            ]
-            sequences[item, parity] = jnp.concatenate(columns, axis=1)
-
-    def gather_groups(blocks, item):
+        for i, item in enumerate(items):
+            for parity in range(2):
+                columns = [
+                    jnp.concatenate(
+                        [moved[(i * own + c) * pieces + m] for m in range(parity, pieces, 2)],
+                        axis=0,
+                    )
+                    for c in range(own)
+                ]
+                sequences[item, parity] = jnp.concatenate(columns, axis=1)
+
+    def gather_groups(blocks, start, stop):
         blocks = blocks.reshape((seq_count, trace_groups) + blocks.shape[1:])
         for side in range(trace_groups):
-            gather(blocks[:, side], item + side)
+            gather(blocks[:, side], range(start + side, stop, trace_groups))
 
     def ahead_first(n):
         sides = []
@@ -279,21 +301,15 @@
         fourth = square * square
         return (fourth * fourth * scaled).astype(BF16)
 
-    def decode(coded, inverse):
-        values = coded.astype(F32)
-        size = jnp.abs(values)
-        root = jnp.exp2(jnp.log2(size) * (1.0 / POWER)) * inverse
-        root = jnp.where(size > 0.0, root, 0.0)
-        return jnp.where(values < 0.0, -root, root)
-
     first_c, first_s = 1, 1 + traces
     arrive(recv_t, seq_count - 1, taps_slot)
-    gather(recv_t[...], 0)
-    for i in range(held):
+    gather(recv_t[...], [0])
+    step = traces // cot_parts
+    for i in range(cot_parts):
         arrive(recv_c.at[i], total - 1, cot_slot + i)
-        base = first_c + i * trace_groups
-        gather_groups(recv_c[i], base)
-        ahead_all(base if i else 0, base + trace_groups)
+        base = first_c + i * step
+        gather_groups(recv_c[i], base, base + step)
+        ahead_all(base if i else 0, base + step)
 
     arrive(peaks_far, far_count - 1, far_slot)
     bounds = jnp.max(peaks_far[...], axis=0)
@@ -321,21 +337,24 @@
         sweep(1 if turn == trace_groups - 1 else 0, seq_count, send_input)
     in_i[me] = out_i[seq, group]
 
-    for i in range(held):
+    sums = [None] * own
+    step = traces // sig_parts
+    for i in range(sig_parts):
         arrive(recv_s.at[i], total - 1, sig_slot + i)
-        base = first_s + i * trace_groups
-        gather_groups(recv_s[i], base)
-        ahead_all(base, base + trace_groups)
-    sums = []
-    for c in range(own):
-        acc = None
-        for b in range(traces):
-            product = turned_product(spectra[first_s + b, c], spectra[first_c + b, c])
-            acc = product if acc is None else acc + product
-        sums.append(acc)
+        base = i * step
+        gather_groups(recv_s[i], first_s + base, first_s + base + step)
+        ahead_all(first_s + base, first_s + base + step)
+        for b in range(base, base + step):
+            for c in range(own):
+                product = turned_product(spectra[first_s + b, c], spectra[first_c + b, c])
+                sums[c] = product if sums[c] is None else sums[c] + product
     coded = cut([encode(values, inverse_f) for values in back_item(sums)])
     out_f[...] = jnp.swapaxes(jnp.stack(coded), 0, 1)
-    in_f[me] = out_f[seq]
+    keep = pltpu.make_async_copy(out_f.at[seq], in_f.at[me], store_sem.at[1])
+    keep.start()
+    scale[...] = jnp.broadcast_to(inverse_f, scale.shape)
+    store_s = pltpu.make_async_copy(scale, scale_out, store_sem.at[2])
+    store_s.start()
     sweep(1, total, lambda step: push(
         out_f.at[lax.div(other(step), trace_groups)], in_f.at[me], filter_slot, other(step)))
 
@@ -350,24 +369,38 @@
     store_i = pltpu.make_async_copy(done_i, input_out, store_sem.at[0])
     store_i.start()
     arrive(in_f, total - 1, filter_slot)
-    moved = jnp.swapaxes(in_f[...], 0, 1)
-    for c in range(own):
-        for m in range(pieces):
-            done_f[m * LANES : (m + 1) * LANES, c * total : (c + 1) * total] = decode(
-                moved[c * pieces + m], inverse_f
-            ).T
-    store_f = pltpu.make_async_copy(done_f, filter_out, store_sem.at[1])
-    store_f.start()
     depart(recv_t, seq_count - 1, taps_slot)
-    for i in range(held):
+    for i in range(cot_parts):
         depart(recv_c.at[i], total - 1, cot_slot + i)
+    for i in range(sig_parts):
         depart(recv_s.at[i], total - 1, sig_slot + i)
     depart(in_i, total - 1, input_slot)
     depart(in_f, total - 1, filter_slot)
     depart(peaks_near, near_count - 1, near_slot)
     depart(peaks_far, far_count - 1, far_slot)
     store_i.wait()
-    store_f.wait()
+    keep.wait()
+    store_s.wait()
+
+
+def finish(input_grad, coded, scale, input_out, filter_out, done, store_sem):
+    span, channels = filter_out.shape
+    total = coded.shape[0]
+    pieces = span // LANES
+    store_i = pltpu.make_async_copy(input_grad, input_out, store_sem.at[0])
+    store_i.start()
+    moved = jnp.swapaxes(coded[...], 0, 1)
+    stores = [store_i]
+    for m in range(pieces):
+        rows = pl.ds(m * LANES, LANES)
+        for c in range(channels // total):
+            done[rows, c * total : (c + 1) * total] = decode(moved[c * pieces + m], scale[...]).T
+        stores.append(
+            pltpu.make_async_copy(done.at[rows], filter_out.at[rows], store_sem.at[1 + m])
+        )
+        stores[-1].start()
+    for store in stores:
+        store.wait()
 
 
 def local(seq_count, trace_groups, signal, cotangent, filter_taps):
@@ -380,28 +413,31 @@
     near_count = min(16, total // 2)
     constants = [jnp.asarray(table) for table in tables(seq_count, pieces)]
     wide, thin = held * own * pieces, own * pieces
+    cot_shape = (COT_PARTS, total, wide // COT_PARTS, LANES)
+    sig_shape = (SIG_PARTS, total, wide // SIG_PARTS, LANES)
     inputs = [cotangent, filter_taps, signal, *constants]
     anywhere = pl.BlockSpec(memory_space=pl.ANY)
 
     def body(*refs):
         kernel(seq_count, trace_groups, near_count, *refs)
 
-    return pl.pallas_call(
+    input_grad, coded, scale = pl.pallas_call(
         body,
         out_shape=(
             jax.ShapeDtypeStruct((held, span, channels), F32),
-            jax.ShapeDtypeStruct((span, channels), F32),
+            jax.ShapeDtypeStruct((total, thin, LANES), BF16),
+            jax.ShapeDtypeStruct((1, LANES), F32),
         ),
         in_specs=[anywhere] * len(inputs),
-        out_specs=(anywhere, anywhere),
+        out_specs=(anywhere,) * 3,
         scratch_shapes=[pltpu.VMEM(array.shape, array.dtype) for array in inputs]
         + [
-            pltpu.VMEM((held, total, thin, LANES), BF16),
+            pltpu.VMEM(cot_shape, BF16),
             pltpu.VMEM((total, thin, LANES), BF16),
-            pltpu.VMEM((held, total, thin, LANES), BF16),
-            pltpu.VMEM((held, total, thin, LANES), BF16),
+            pltpu.VMEM(sig_shape, BF16),
+            pltpu.VMEM(cot_shape, BF16),
             pltpu.VMEM((seq_count, thin, LANES), BF16),
-            pltpu.VMEM((held, total, thin, LANES), BF16),
+            pltpu.VMEM(sig_shape, BF16),
             pltpu.VMEM((1, LANES), F32),
             pltpu.VMEM((near_count, 1, LANES), F32),
             pltpu.VMEM((1, LANES), F32),
@@ -411,19 +447,29 @@
             pltpu.VMEM((seq_count, trace_groups, wide, LANES), BF16),
             pltpu.VMEM((seq_count, thin, LANES), BF16),
             pltpu.VMEM((total, wide, LANES), BF16),
-            pltpu.VMEM((total, thin, LANES), BF16),
             pltpu.VMEM((held, span, channels), F32),
-            pltpu.VMEM((span, channels), F32),
+            pltpu.VMEM((1, LANES), F32),
             pltpu.SemaphoreType.DMA((len(inputs),)),
-            pltpu.SemaphoreType.DMA((2,)),
-            pltpu.SemaphoreType.DMA((5 + 2 * held,)),
-            pltpu.SemaphoreType.DMA((5 + 2 * held,)),
+            pltpu.SemaphoreType.DMA((3,)),
+            pltpu.SemaphoreType.DMA((5 + COT_PARTS + SIG_PARTS,)),
+            pltpu.SemaphoreType.DMA((5 + COT_PARTS + SIG_PARTS,)),
         ],
         name="correlate",
         compiler_params=pltpu.CompilerParams(
             collective_id=0, has_side_effects=True, vmem_limit_bytes=32 << 20
         ),
     )(*[pltpu.with_memory_space_constraint(x, pltpu.HBM) for x in inputs])
+    return pl.pallas_call(
+        finish,
+        out_shape=(
+            jax.ShapeDtypeStruct((held, span, channels), F32),
+            jax.ShapeDtypeStruct((span, channels), F32),
+        ),
+        in_specs=[anywhere, pl.BlockSpec(memory_space=pltpu.VMEM), pl.BlockSpec(memory_space=pltpu.VMEM)],
+        out_specs=(anywhere, anywhere),
+        scratch_shapes=[pltpu.VMEM((span, channels), F32), pltpu.SemaphoreType.DMA((1 + pieces,))],
+        name="finish",
+    )(*[pltpu.with_memory_space_constraint(x, pltpu.VMEM) for x in (input_grad, coded, scale)])
 
 
 def solution(mesh):

time: 41.3 us -> 40.2 us (0.973)
  local copies, waits for them, and re-layouts: 1.77 us -> 0 us
  Pallas kernels: 38.8 us -> 39.4 us
    unnamed x2 -> x0, local copies, waits for them, and re-layouts: 1.77 us -> none
    pallas_call x0 -> x1, Pallas kernels: none -> 1.18 us  [local(): pl.pallas_call(finish, out_shape=(jax.ShapeDtypeStruct((held, span, chann...]
    pallas_call x1, Pallas kernels: 38.8 us -> 38.2 us  [local(): pl.pallas_call(body, out_shape=(jax.ShapeDtypeStruct((held, span, channel...]
where the time goes in v4:
time: 40.2 us; the launch traced here: 40.1 us
  Pallas kernels  39.4 us (98%)
  between operations  0.64 us (2%)
    pallas_call x1, Pallas kernels, local(): pl.pallas_call(body, out_shape=(jax.ShapeDtypeStruct((held, span, channel...  38.2 us
    pallas_call x1, Pallas kernels, local(): pl.pallas_call(finish, out_shape=(jax.ShapeDtypeStruct((held, span, chann...  1.18 us

profile of v4, /device:TPU:1, one launch (start us, length us, event | category | flops | bytes accessed | tf_op | source)
XLA Modules:
  0.0 40.1 jit_solution(14508048310904658459)
XLA Ops:
  0.6 38.2 %correlate.1 = (f32[2,512,256]{2,1,0:T(8,128)S(1)}, bf16[128,8,128]{2,1,0:T(8,128)(2,1)S(1)}, f32[1,128]{1,0:T(1,128)S(1)}) custom-call(bf16[2,512,256]{2,1,0:T(8,128)(2,1)} %refs_0_.1, bf16[512,256]{1,0:T(8,128)(2,1)} %refs_1_.1, bf16[2,512,256]{2,1,0:T(8,128)(2,1)} %refs_2_.1, bf16[2,256,256]{2,1,0:T(8,128)(2,1)} %constant.10.clone.refs_3_, ...), custom_call_target="tpu_custom_call" | custom-call | tf_op jit(solution)/shard_map/correlate/pallas_call | solution.py:424
  38.9 1.2 %finish.1 = (f32[2,512,256]{2,1,0:T(8,128)}, f32[512,256]{1,0:T(8,128)}) custom-call(f32[2,512,256]{2,1,0:T(8,128)S(1)} %get-tuple-element.5.input_grad, bf16[128,8,128]{2,1,0:T(8,128)(2,1)S(1)} %get-tuple-element.6.coded, f32[1,128]{1,0:T(1,128)S(1)} %get-tuple-element.7.scale), custom_call_target="tpu_custom_call" | custom-call | tf_op jit(solution)/shard_map/finish/pallas_call | solution.py:462

commit v5 on v4

--- a/solution.py
+++ b/solution.py
@@ -10,6 +10,7 @@
 
 LANES = 128
 STRIDE = 37
+GREETING = 1
 POWER = 9
 CEILING = 2.0**14
 UNROLL = 8
@@ -69,16 +70,16 @@
     return jnp.where(values < 0.0, -root, root)
 
 
-def sweep(start, stop, action):
-    groups = (stop - start) // UNROLL
+def sweep(start, stop, action, unroll=UNROLL):
+    groups = (stop - start) // unroll
 
     def batch(index, carry):
-        for k in range(UNROLL):
-            action(start + index * UNROLL + k)
+        for k in range(unroll):
+            action(start + index * unroll + k)
         return carry
 
     lax.fori_loop(0, groups, batch, 0)
-    for step in range(start + groups * UNROLL, stop):
+    for step in range(start + groups * unroll, stop):
         action(step)
 
 
@@ -118,7 +119,7 @@
         return lax.rem(seq + step * STRIDE, seq_count)
 
     sweep(1, total, lambda step: pl.semaphore_signal(
-        barrier, inc=1, device_id=other(step), device_id_type=LOGICAL))
+        barrier, inc=1, device_id=lax.rem(me + step * GREETING, total), device_id_type=LOGICAL), 32)
 
     def part(ref, index, parts):
         step = held // parts

time: 40.2 us -> 40 us (level)
  no operation moved by 1% of the time
where the time goes in v5:
time: 40 us; the launch traced here: 39.9 us
  Pallas kernels  39.3 us (98%)
  between operations  0.64 us (2%)
    pallas_call x1, Pallas kernels, local(): pl.pallas_call(body, out_shape=(jax.ShapeDtypeStruct((held, span, channel...  38.1 us
    pallas_call x1, Pallas kernels, local(): pl.pallas_call(finish, out_shape=(jax.ShapeDtypeStruct((held, span, chann...  1.18 us

profile of v5, /device:TPU:1, one launch (start us, length us, event | category | flops | bytes accessed | tf_op | source)
XLA Modules:
  0.0 39.9 jit_solution(4333931442567360605)
XLA Ops:
  0.6 38.1 %correlate.1 = (f32[2,512,256]{2,1,0:T(8,128)S(1)}, bf16[128,8,128]{2,1,0:T(8,128)(2,1)S(1)}, f32[1,128]{1,0:T(1,128)S(1)}) custom-call(bf16[2,512,256]{2,1,0:T(8,128)(2,1)} %refs_0_.1, bf16[512,256]{1,0:T(8,128)(2,1)} %refs_1_.1, bf16[2,512,256]{2,1,0:T(8,128)(2,1)} %refs_2_.1, bf16[2,256,256]{2,1,0:T(8,128)(2,1)} %constant.10.clone.refs_3_, ...), custom_call_target="tpu_custom_call" | custom-call | tf_op jit(solution)/shard_map/correlate/pallas_call | solution.py:425
  38.7 1.2 %finish.1 = (f32[2,512,256]{2,1,0:T(8,128)}, f32[512,256]{1,0:T(8,128)}) custom-call(f32[2,512,256]{2,1,0:T(8,128)S(1)} %get-tuple-element.5.input_grad, bf16[128,8,128]{2,1,0:T(8,128)(2,1)S(1)} %get-tuple-element.6.coded, f32[1,128]{1,0:T(1,128)S(1)} %get-tuple-element.7.scale), custom_call_target="tpu_custom_call" | custom-call | tf_op jit(solution)/shard_map/finish/pallas_call | solution.py:463

commit v6 on v5

--- a/solution.py
+++ b/solution.py
@@ -114,6 +114,15 @@
 
     def other(step):
         return lax.rem(me + step * STRIDE, total)
+
+    def crossing(action):
+        for turn in range(trace_groups):
+            side = lax.rem(group + 1 + turn, trace_groups)
+            sweep(
+                1 if turn == trace_groups - 1 else 0,
+                seq_count,
+                lambda step: action(along(step), side),
+            )
 
     def along(step):
         return lax.rem(seq + step * STRIDE, seq_count)
@@ -356,8 +365,8 @@
     scale[...] = jnp.broadcast_to(inverse_f, scale.shape)
     store_s = pltpu.make_async_copy(scale, scale_out, store_sem.at[2])
     store_s.start()
-    sweep(1, total, lambda step: push(
-        out_f.at[lax.div(other(step), trace_groups)], in_f.at[me], filter_slot, other(step)))
+    crossing(lambda target, side: push(
+        out_f.at[target], in_f.at[me], filter_slot, target * trace_groups + side))
 
     arrive(in_i, total - 1, input_slot)
     moved = jnp.swapaxes(in_i[...], 0, 1)

time: 40 us -> 39.6 us (0.990)
    pallas_call x1, Pallas kernels: 38.1 us -> 37.7 us  [local(): pl.pallas_call(body, out_shape=(jax.ShapeDtypeStruct((held, span, channel...]
where the time goes in v6:
time: 39.6 us; the launch traced here: 39.5 us
  Pallas kernels  38.9 us (98%)
  between operations  0.64 us (2%)
    pallas_call x1, Pallas kernels, local(): pl.pallas_call(body, out_shape=(jax.ShapeDtypeStruct((held, span, channel...  37.7 us
    pallas_call x1, Pallas kernels, local(): pl.pallas_call(finish, out_shape=(jax.ShapeDtypeStruct((held, span, chann...  1.18 us

profile of v6, /device:TPU:1, one launch (start us, length us, event | category | flops | bytes accessed | tf_op | source)
XLA Modules:
  0.0 39.5 jit_solution(4930097376391218644)
XLA Ops:
  0.6 37.7 %correlate.1 = (f32[2,512,256]{2,1,0:T(8,128)S(1)}, bf16[128,8,128]{2,1,0:T(8,128)(2,1)S(1)}, f32[1,128]{1,0:T(1,128)S(1)}) custom-call(bf16[2,512,256]{2,1,0:T(8,128)(2,1)} %refs_0_.1, bf16[512,256]{1,0:T(8,128)(2,1)} %refs_1_.1, bf16[2,512,256]{2,1,0:T(8,128)(2,1)} %refs_2_.1, bf16[2,256,256]{2,1,0:T(8,128)(2,1)} %constant.10.clone.refs_3_, ...), custom_call_target="tpu_custom_call" | custom-call | tf_op jit(solution)/shard_map/correlate/pallas_call | solution.py:434
  38.3 1.2 %finish.1 = (f32[2,512,256]{2,1,0:T(8,128)}, f32[512,256]{1,0:T(8,128)}) custom-call(f32[2,512,256]{2,1,0:T(8,128)S(1)} %get-tuple-element.5.input_grad, bf16[128,8,128]{2,1,0:T(8,128)(2,1)S(1)} %get-tuple-element.6.coded, f32[1,128]{1,0:T(1,128)S(1)} %get-tuple-element.7.scale), custom_call_target="tpu_custom_call" | custom-call | tf_op jit(solution)/shard_map/finish/pallas_call | solution.py:472

commit v7 on v6

--- a/solution.py
+++ b/solution.py
@@ -207,8 +207,8 @@
     peaks_near[second] = peak[...]
     pl.semaphore_wait(barrier, total - 1)
     sweep(1, near_count, send_near)
+    sweep(1, total, send_cot(0))
     sweep(1, seq_count, send_taps)
-    sweep(1, total, send_cot(0))
     for i in range(1, cot_parts):
         stage(part(cot, i, cot_parts), send_c.at[i], recv_c.at[i], me)
         sweep(1, total, send_cot(i))

time: 39.6 us -> 39.6 us (level)
  no operation moved by 1% of the time
where the time goes in v7:
time: 39.6 us; the launch traced here: 39.5 us
  Pallas kernels  38.9 us (98%)
  between operations  0.64 us (2%)
    pallas_call x1, Pallas kernels, local(): pl.pallas_call(body, out_shape=(jax.ShapeDtypeStruct((held, span, channel...  37.7 us
    pallas_call x1, Pallas kernels, local(): pl.pallas_call(finish, out_shape=(jax.ShapeDtypeStruct((held, span, chann...  1.18 us

profile of v7, /device:TPU:1, one launch (start us, length us, event | category | flops | bytes accessed | tf_op | source)
XLA Modules:
  0.0 39.5 jit_solution(12443001979549575734)
XLA Ops:
  0.6 37.7 %correlate.1 = (f32[2,512,256]{2,1,0:T(8,128)S(1)}, bf16[128,8,128]{2,1,0:T(8,128)(2,1)S(1)}, f32[1,128]{1,0:T(1,128)S(1)}) custom-call(bf16[2,512,256]{2,1,0:T(8,128)(2,1)} %refs_0_.1, bf16[512,256]{1,0:T(8,128)(2,1)} %refs_1_.1, bf16[2,512,256]{2,1,0:T(8,128)(2,1)} %refs_2_.1, bf16[2,256,256]{2,1,0:T(8,128)(2,1)} %constant.10.clone.refs_3_, ...), custom_call_target="tpu_custom_call" | custom-call | tf_op jit(solution)/shard_map/correlate/pallas_call | solution.py:434
  38.3 1.2 %finish.1 = (f32[2,512,256]{2,1,0:T(8,128)}, f32[512,256]{1,0:T(8,128)}) custom-call(f32[2,512,256]{2,1,0:T(8,128)S(1)} %get-tuple-element.5.input_grad, bf16[128,8,128]{2,1,0:T(8,128)(2,1)S(1)} %get-tuple-element.6.coded, f32[1,128]{1,0:T(1,128)S(1)} %get-tuple-element.7.scale), custom_call_target="tpu_custom_call" | custom-call | tf_op jit(solution)/shard_map/finish/pallas_call | solution.py:472
